TPU v7x, 128 devices: a whole 4x4x4 slice. The times are simulated.
128 devices in a mesh: gz: 32 (over y, z_hi, x), xy: 4 (over z_lo, core).
Axes of the slice: x: 4, y: 4, z: 4 (z_hi: 2, z_lo: 2; z = z_hi * 2 + z_lo), core: 2. Of those that a mesh axis runs over, the one named last changes fastest.
Arguments:
- raw_volume: bfloat16 [64, 512, 512], P('gz', 'xy'), may hold values from -6 to 6
- weight_first: bfloat16 [32, 1, 3, 3], replicated, may hold values from -3 to 3
- bias_first: float32 [32], replicated, may hold values from -3 to 3
- weight_second: bfloat16 [64, 32, 3, 3], replicated, may hold values from -0.5 to 0.5
- bias_second: float32 [64], replicated, may hold values from -3 to 3
- weight_third: bfloat16 [128, 64, 3, 3], replicated, may hold values from -0.375 to 0.375
- bias_third: float32 [128], replicated, may hold values from -3 to 3
- weight_iso_a: bfloat16 [3, 3, 3, 128, 256], replicated, may hold values from -0.15625 to 0.15625
- bias_iso_a: float32 [256], replicated, may hold values from -3 to 3
- weight_iso_b: bfloat16 [3, 3, 3, 256, 256], replicated, may hold values from -0.109375 to 0.109375
- bias_iso_b: float32 [256], replicated, may hold values from -3 to 3
Outputs:
- features: bfloat16 [64, 64, 64, 256], P(None, 'xy', 'gz')
All inputs are finite; a program needn't handle non-finite values.
Results may differ from a plain program's by a relative error of at most 0.0069.
Values may be sent and summed in bfloat16 or wider, within the bound.
A program may use at most 128 MiB of HBM per device.

v0:
```python
import functools

import jax
import jax.numpy as jnp
from jax import lax
from jax.experimental import pallas as pl
from jax.experimental.pallas import tpu as pltpu
from jax.sharding import PartitionSpec as P

F32 = jnp.float32
BF16 = jnp.bfloat16
MESH = pl.DeviceIdType.MESH
VMEM = pl.BlockSpec(memory_space=pltpu.VMEM)
ANY = pl.BlockSpec(memory_space=pl.ANY)
ROWS = 168
WINS = 10


def picker():
    source = lax.broadcasted_iota(jnp.int32, (512, 1280), 0)
    column = lax.broadcasted_iota(jnp.int32, (512, 1280), 1)
    j, m = column // 128, column % 128
    x2 = 2 * (m % 64) + m // 64
    return (source == 4 * x2 - 3 + j).astype(BF16)


def banded_first(weight):
    taps = jnp.tile(jnp.transpose(weight[:, 0], (1, 2, 0)), (1, 1, 8))
    lane = lax.broadcasted_iota(jnp.int32, (10, 256), 1)
    j = lax.broadcasted_iota(jnp.int32, (10, 256), 0)
    first = 2 * ((lane // 32) % 4) + lane // 128
    rows = lax.broadcasted_iota(jnp.int32, (16, 10, 24, 256), 2)
    step = lax.broadcasted_iota(jnp.int32, (16, 10, 24, 256), 0)
    total = jnp.zeros((16, 10, 24, 256), BF16)
    for ky in range(3):
        cols = jnp.zeros((10, 256), BF16)
        for kx in range(3):
            cols = jnp.where(j == first + kx, taps[ky, kx][None, :], cols)
        total = jnp.where(rows == step + 1 + ky, cols[None, :, None, :], total)
    return jnp.pad(total.reshape(16, 240, 256), ((0, 0), (0, 16), (0, 0)))


def banded_second(weight):
    taps = jnp.transpose(weight, (2, 3, 1, 0))
    parts = [
        jnp.pad(taps, ((py, 1 - py), (px, 1 - px), (0, 0), (0, 0))).reshape(512, 64)
        for py in range(2)
        for px in range(2)
    ]
    return jnp.concatenate(parts, axis=1)


def banded_third(weight):
    taps = jnp.transpose(weight, (2, 3, 1, 0))
    parts = [jnp.pad(taps, ((0, 0), (px, 1 - px), (0, 0), (0, 0))).reshape(768, 128) for px in range(2)]
    return jnp.concatenate(parts, axis=1)


def plane_kernel(raw, pick, w1, b1, w2, b2, w3, b3, out, spread, turned, first, second, third):
    yi = lax.axis_index("xy")
    ny = lax.axis_size("xy")
    lane = lax.broadcasted_iota(jnp.int32, (128, 128), 1)
    sub = lax.broadcasted_iota(jnp.int32, (128, 128), 0)
    inside = jnp.logical_not(
        jnp.logical_or(
            jnp.logical_and(sub == 0, lane < 32), jnp.logical_and(sub == 127, lane >= 96)
        )
    )
    inside_f = jnp.where(inside, 1.0, 0.0)
    lane64 = lax.broadcasted_iota(jnp.int32, (64, 128), 1)
    sub64 = lax.broadcasted_iota(jnp.int32, (64, 128), 0)

    @pl.loop(0, 2)
    def _(z):
        spread[...] = jnp.dot(raw[z], pick[...], preferred_element_type=F32)

        @pl.loop(0, WINS)
        def _(w):
            rows = pl.ds(pl.multiple_of(w * 16, 16), 24)
            parts = [spread[rows, j * 128 : (j + 1) * 128] for j in range(10)]
            parts.append(jnp.zeros((16, 128), F32))
            turned[w] = jnp.concatenate(parts, axis=0).T.astype(BF16)

        @pl.loop(0, 8)
        def _(i):
            for w0 in range(0, WINS, 2):
                lhs = turned[w0 : w0 + 2].reshape(256, 256)
                one = jnp.dot(lhs, w1[2 * i], preferred_element_type=F32)
                two = jnp.dot(lhs, w1[2 * i + 1], preferred_element_type=F32)
                top = jnp.maximum(one, two)
                top = jnp.maximum(top[:, :128], top[:, 128:])
                top = jnp.maximum(top + b1[...], 0.0).reshape(2, 128, 128)
                for k in range(2):
                    row = 8 * (w0 + k) + i
                    place = 64 * yi + row - 7
                    valid = jnp.logical_and(place >= 0, place < 64 * ny)
                    scale = inside_f * jnp.where(valid, 1.0, 0.0)
                    first[row] = (top[k] * scale).astype(BF16)

        @pl.loop(0, 19)
        def _(g):
            base = 4 * g
            lhs = jnp.concatenate(
                [
                    jnp.concatenate([first[base + 2 * k + a] for a in range(4)], axis=1)
                    for k in range(2)
                ],
                axis=0,
            )
            res = jnp.dot(lhs, w2[...], preferred_element_type=F32)
            top = jnp.maximum(res[:, :128], res[:, 128:])
            top = jnp.maximum(top, pltpu.roll(top, 64, 1))
            top = jnp.maximum(top + b2[...], 0.0)
            for k in range(2):
                q = 2 * g + k
                place = 32 * yi + q - 3
                valid = jnp.logical_and(place >= 0, place < 32 * ny)
                val = top[128 * k : 128 * k + 128] * jnp.where(valid, 1.0, 0.0)
                even, odd = val[:64], val[64:]
                down = jnp.where(sub64 == 0, 0.0, pltpu.roll(odd, 1, 0))
                up = jnp.where(sub64 == 63, 0.0, pltpu.roll(even, 63, 0))
                second[q, :, :128] = jnp.where(lane64 < 64, down, even).astype(BF16)
                second[q, :, 128:] = jnp.where(lane64 < 64, odd, up).astype(BF16)

        @pl.loop(0, 9)
        def _(g):
            base = 4 * g
            lhs = jnp.concatenate(
                [second[pl.ds(base + ky, 4)].reshape(256, 256) for ky in range(3)], axis=1
            )
            res = jnp.dot(lhs, w3[...], preferred_element_type=F32)
            top = jnp.maximum(res[:, :128], res[:, 128:]).reshape(2, 2, 64, 128)
            top = jnp.maximum(top[:, 0], top[:, 1])
            top = jnp.maximum(top + b3[...], 0.0)
            for k in range(2):
                t = 2 * g + k
                place = 16 * yi + t - 1
                valid = jnp.logical_and(place >= 0, place < 16 * ny)
                third[t] = top[k] * jnp.where(valid, 1.0, 0.0)

        for t in range(18, 24):
            third[t] = jnp.zeros((64, 128), F32)
        out[0, z] = jnp.zeros((24, 128), BF16)
        out[65, z] = jnp.zeros((24, 128), BF16)

        @pl.loop(0, 8)
        def _(g):
            x0 = pl.multiple_of(8 * g, 8)
            block = third[:, pl.ds(x0, 8), :]
            out[pl.ds(1 + x0, 8), z] = jnp.transpose(block, (1, 0, 2)).astype(BF16)


def plane_levels(raw, pick, w1, b1, w2, b2, w3, b3):
    return pl.pallas_call(
        plane_kernel,
        name="plane_levels",
        out_shape=jax.ShapeDtypeStruct((66, 2, 24, 128), BF16),
        in_specs=[VMEM] * 8,
        out_specs=VMEM,
        scratch_shapes=[
            pltpu.VMEM((ROWS, 1280), F32),
            pltpu.VMEM((WINS, 128, 256), BF16),
            pltpu.VMEM((80, 128, 128), BF16),
            pltpu.VMEM((38, 64, 256), BF16),
            pltpu.VMEM((24, 64, 128), F32),
        ],
        compiler_params=pltpu.CompilerParams(vmem_limit_bytes=40 << 20),
    )(raw, pick, w1, b1, w2, b2, w3, b3)


def turn_kernel(peers, slab, brick, send_sem, recv_sem, local_sem):
    me = lax.axis_index("gz")
    yi = lax.axis_index("xy")

    barrier = pltpu.get_barrier_semaphore()

    @pl.loop(1, peers)
    def _(k):
        pl.semaphore_signal(
            barrier, inc=1, device_id=(lax.rem(me + k, peers), yi), device_id_type=MESH
        )

    pl.semaphore_wait(barrier, peers - 1)

    def copy(k):
        there = lax.rem(me + k, peers)
        return pltpu.make_async_remote_copy(
            src_ref=slab.at[pl.ds(2 * there, 4)],
            dst_ref=brick.at[:, pl.ds(2 * me, 2)],
            send_sem=send_sem.at[k],
            recv_sem=recv_sem.at[k],
            device_id=(there, yi),
            device_id_type=MESH,
        )

    own = pltpu.make_async_copy(
        slab.at[pl.ds(2 * me, 4)], brick.at[:, pl.ds(2 * me, 2)], local_sem
    )
    own.start()

    @pl.loop(1, peers)
    def _(k):
        copy(k).start()

    own.wait()

    @pl.loop(1, peers)
    def _(k):
        copy(k).wait()


def turn(slab, peers):
    return pl.pallas_call(
        functools.partial(turn_kernel, peers),
        name="turn",
        out_shape=jax.ShapeDtypeStruct((4, 2 * peers, 24, 128), BF16),
        in_specs=[VMEM],
        out_specs=VMEM,
        scratch_shapes=[
            pltpu.SemaphoreType.DMA((peers,)),
            pltpu.SemaphoreType.DMA((peers,)),
            pltpu.SemaphoreType.DMA,
        ],
        compiler_params=pltpu.CompilerParams(collective_id=0, has_side_effects=True),
    )(slab)


def cube_kernel(depth, chans, brick, weight, bias, out, tall):
    for ky in range(3):
        for x in range(4):
            tall[ky, x, 0] = jnp.zeros((16, chans), BF16)
            tall[ky, x, depth + 1] = jnp.zeros((16, chans), BF16)

    @pl.loop(0, depth)
    def _(z):
        for x in range(4):
            rows = brick[x, z].astype(F32)
            for ky in range(3):
                tall[ky, x, z + 1] = rows[ky : ky + 16].astype(BF16)

    step = 16
    for x in range(2):

        @pl.loop(0, depth // step)
        def _(g):
            z0 = g * step
            lhs = jnp.concatenate(
                [
                    tall[ky, x + kx, pl.ds(z0 + kz, step)].reshape(step * 16, chans)
                    for kz in range(3)
                    for ky in range(3)
                    for kx in range(3)
                ],
                axis=1,
            )
            res = jnp.dot(lhs, weight[...], preferred_element_type=F32)
            res = jnp.maximum(res + bias[...], 0.0).astype(BF16)
            out[x, pl.ds(z0, step)] = res.reshape(step, 16, 256)


def cube(brick, weight, bias):
    _, depth, _, chans = brick.shape
    return pl.pallas_call(
        functools.partial(cube_kernel, depth, chans),
        name="cube",
        out_shape=jax.ShapeDtypeStruct((2, depth, 16, 256), BF16),
        in_specs=[VMEM] * 3,
        out_specs=VMEM,
        scratch_shapes=[pltpu.VMEM((3, 4, depth + 2, 16, chans), BF16)],
        compiler_params=pltpu.CompilerParams(vmem_limit_bytes=56 << 20),
    )(brick, weight.reshape(27 * chans, 256), bias.reshape(1, 256))


def shift(block, axis, forward):
    count = lax.axis_size(axis)
    pairs = [(i, i + 1) for i in range(count - 1)]
    if not forward:
        pairs = [(b, a) for a, b in pairs]
    return lax.ppermute(block, axis, pairs)


def body(raw, wf, bf, ws, bs, wt, bt, wa, ba, wb, bb):
    low = shift(raw[:, 112:], "xy", True)
    high = shift(raw[:, :16], "xy", False)
    padded = jnp.concatenate([low, raw, high, jnp.zeros((2, 8, 512), BF16)], axis=1)
    slab = plane_levels(
        padded,
        picker(),
        banded_first(wf),
        jnp.tile(bf, 4).reshape(1, 128),
        banded_second(ws),
        jnp.tile(bs, 2).reshape(1, 128),
        banded_third(wt),
        bt.reshape(1, 128),
    )
    brick = turn(slab, lax.axis_size("gz"))
    middle = cube(brick, wa, ba)
    above = shift(middle[:, :, 15:], "xy", True)
    below = shift(middle[:, :, :1], "xy", False)
    middle = jnp.concatenate([above, middle, below, jnp.zeros((2, 64, 6, 256), BF16)], axis=2)
    left = shift(middle[1:], "gz", True)
    right = shift(middle[:1], "gz", False)
    out = cube(jnp.concatenate([left, middle, right], axis=0), wb, bb)
    return jnp.transpose(out, (1, 2, 0, 3))


def solution(mesh):
    placed = (P("gz", "xy", None), P(), P(), P(), P(), P(), P(), P(), P(), P(), P())
    return jax.shard_map(
        body, mesh=mesh, in_specs=placed, out_specs=P(None, "xy", "gz", None), check_vma=False
    )
```

profile of v0, /device:TPU:31, one launch (start us, length us, event | category | flops | bytes accessed | tf_op | source)
XLA Modules:
  0.0 145.6 jit_solution(17915421394586355948)
XLA Ops:
  0.0 0.8 fusion.23
  0.8 4.1 %collective-permute-start = (bf16[2,16,512]{2,1,0:T(8,128)(2,1)S(1)}, bf16[2,16,512]{2,1,0:T(8,128)(2,1)S(1)}, u32[]{:S(2)}, u32[]{:S(2)}) collective-permute-start(bf16[2,16,512]{2,1,0:T(8,128)(2,1)S(1)} %get-tuple-element.18), channel_id=1, source_target_pairs={{0,1},{1,2},{2,3},{4,5},{5,6},{6,7},{8,9},{9,10},{10,11},{12,13},{... | collective-permute-start | bytes 98312 | tf_op jit(solution)/shard_map/ppermute | solution.py:279
  4.9 1.9 %collective-permute-start.1 = (bf16[2,16,512]{2,1,0:T(8,128)(2,1)S(1)}, bf16[2,16,512]{2,1,0:T(8,128)(2,1)S(1)}, u32[]{:S(2)}, u32[]{:S(2)}) collective-permute-start(bf16[2,16,512]{2,1,0:T(8,128)(2,1)S(1)} %get-tuple-element.19), channel_id=1, source_target_pairs={{1,0},{2,1},{3,2},{5,4},{6,5},{7,6},{9,8},{10,9},{11,10},{13,12},{... | collective-permute-start | bytes 98312 | tf_op jit(solution)/shard_map/ppermute | solution.py:279
  6.9 0.7 tile.8
  7.6 0.1 tile.9
  7.7 0.1 iota.226
  7.8 1.1 fusion.25
  9.0 1.0 fusion.24
  10.1 0.0 copy-start.4
  10.1 0.0 copy-start.5
  10.1 0.4 fusion.10.pick
  10.6 2.3 %compare_select_fusion.2 = bf16[16,240,256]{2,1,0:T(8,128)(2,1)} fusion(s32[16]{0:T(128)S(1)} %get-tuple-element.41, s32[16]{0:T(128)S(1)} %get-tuple-element.42, s32[16]{0:T(128)S(1)} %iota_add_fusion.2, s32[240]{0:T(256)S(1)} %iota.226, bf16[240,256]{1,0:T(8,128)(2,1)S(1)} %bitcast.34, bf16[240,256]{1,0:T(8,128)(2,1)S(1)} %bitcast.33, ...), kind=kLoop, calls=%fused_computation.10 | loop fusion | flops 5898240 | bytes 2335872 | tf_op jit(solution)/shard_map/jit(_where)/select_n | solution.py:39
  12.9 0.0 copy-start.3
  12.9 0.0 copy-start.1
  12.9 0.2 pad_maximum_fusion.3.w2
  13.1 0.0 copy-done.4
  13.1 0.1 reshape_tile.6.b1
  13.2 0.0 copy-done.5
  13.2 0.1 reshape_tile.7.b2
  13.3 1.8 %pad.28.w1 = bf16[16,256,256]{2,1,0:T(8,128)(2,1)S(1)} pad(bf16[16,240,256]{2,1,0:T(8,128)(2,1)} %compare_select_fusion.2, bf16[]{:T(256)} %constant.94.clone.1), padding=0_0x0_16x0_0 | pad | bytes 4063234 | tf_op jit(solution)/shard_map/jit(_pad)/pad | solution.py:40
  15.0 0.1 pad.54.clone
  15.1 0.0 collective-permute-done
  15.1 0.0 collective-permute-done.1
  15.1 0.0 copy-done.3
  15.1 0.1 maximum_maximum_fusion.raw
  15.3 0.0 copy-done.1
  15.3 28.2 %plane_levels.1.slab = bf16[66,2,24,128]{3,2,1,0:T(8,128)(2,1)S(1)} custom-call(bf16[2,168,512]{2,1,0:T(8,128)(2,1)S(1)} %maximum_maximum_fusion.raw, bf16[512,1280]{1,0:T(8,128)(2,1)S(1)} %fusion.10.pick, bf16[16,256,256]{2,1,0:T(8,128)(2,1)S(1)} %pad.28.w1, f32[1,128]{1,0:T(1,128)S(1)} %reshape_tile.6.b1, bf16[512,256]{1,0:T(8,128)(2,1)S(1)} %pad_maximum_fusion.3.w2, ...), custom_call_target="tpu_custom_call" | custom-call | tf_op jit(solution)/shard_map/plane_levels/pallas_call | solution.py:154
  43.5 0.0 copy-start
  43.5 0.9 copy-done
  44.4 29.8 %turn.1.brick = bf16[4,64,24,128]{3,2,1,0:T(8,128)(2,1)} custom-call(bf16[66,2,24,128]{3,2,1,0:T(8,128)(2,1)} %copy-done), custom_call_target="tpu_custom_call" | custom-call | tf_op jit(solution)/shard_map/turn/pallas_call | solution.py:213
  74.1 9.3 %cube.2 = bf16[2,64,16,256]{3,2,1,0:T(8,128)(2,1)} custom-call(bf16[4,64,24,128]{3,2,1,0:T(8,128)(2,1)} %turn.1.brick, bf16[3456,256]{1,0:T(8,128)(2,1)} %bitcast.25, f32[1,256]{1,0:T(1,128)} %bitcast.38), custom_call_target="tpu_custom_call" | custom-call | tf_op jit(solution)/shard_map/cube/pallas_call | solution.py:263
  83.4 1.4 fusion.22
  84.8 3.3 %collective-permute-start.2 = (bf16[2,64,1,256]{3,2,1,0:T(2,128)(2,1)S(1)}, bf16[2,64,1,256]{3,2,1,0:T(2,128)(2,1)S(1)}, u32[]{:S(2)}, u32[]{:S(2)}) collective-permute-start(bf16[2,64,1,256]{3,2,1,0:T(2,128)(2,1)S(1)} %get-tuple-element.16), channel_id=1, source_target_pairs={{0,1},{1,2},{2,3},{4,5},{5,6},{6,7},{8,9},{9,10},{10,11},{12,13},{... | collective-permute-start | bytes 196616 | tf_op jit(solution)/shard_map/ppermute | solution.py:279
  88.2 1.9 %collective-permute-start.3 = (bf16[2,64,1,256]{3,2,1,0:T(2,128)(2,1)S(1)}, bf16[2,64,1,256]{3,2,1,0:T(2,128)(2,1)S(1)}, u32[]{:S(2)}, u32[]{:S(2)}) collective-permute-start(bf16[2,64,1,256]{3,2,1,0:T(2,128)(2,1)S(1)} %get-tuple-element.17), channel_id=1, source_target_pairs={{1,0},{2,1},{3,2},{5,4},{6,5},{7,6},{9,8},{10,9},{11,10},{13,12},{... | collective-permute-start | bytes 196616 | tf_op jit(solution)/shard_map/ppermute | solution.py:279
  90.1 0.0 collective-permute-done.2
  90.1 4.3 %collective-permute-done.3 = bf16[2,64,1,256]{3,2,1,0:T(2,128)(2,1)S(1)} collective-permute-done((bf16[2,64,1,256]{3,2,1,0:T(2,128)(2,1)S(1)}, bf16[2,64,1,256]{3,2,1,0:T(2,128)(2,1)S(1)}, u32[]{:S(2)}, u32[]{:S(2)}) %collective-permute-start.3) | collective-permute-done | bytes 65568 | tf_op jit(solution)/shard_map/ppermute | solution.py:279
  94.5 0.0 copy-start.2
  94.5 2.7 %pad_maximum_fusion.1 = bf16[2,64,24,256]{3,2,1,0:T(8,128)(2,1)S(1)} fusion(bf16[2,64,6,256]{3,2,1,0:T(8,128)(2,1)S(1)} %broadcast_in_dim.137, bf16[2,64,1,256]{3,2,1,0:T(2,128)(2,1)S(1)} %collective-permute-done.3, bf16[2,64,16,256]{3,2,1,0:T(8,128)(2,1)} %cube.2, bf16[2,64,1,256]{3,2,1,0:T(2,128)(2,1)S(1)} %collective-permute-done.2), kind=kLoop, calls=%fused_computation.23 | loop fusion | flops 6291456 | bytes 3145728 | tf_op jit(solution)/shard_map/concatenate | solution.py:300
  97.2 0.1 fusion.21
  97.3 5.8 %collective-permute-start.4 = (bf16[1,64,24,256]{3,2,1,0:T(8,128)(2,1)S(1)}, bf16[1,64,24,256]{3,2,1,0:T(8,128)(2,1)S(1)}, u32[]{:S(2)}, u32[]{:S(2)}) collective-permute-start(bf16[1,64,24,256]{3,2,1,0:T(8,128)(2,1)S(1)} %get-tuple-element.14), channel_id=1, source_target_pairs={{0,4},{4,8},{8,12},{12,16},{16,20},{20,24},{24,28},{28,32},{32,36}... | collective-permute-start | bytes 2359304 | tf_op jit(solution)/shard_map/ppermute | solution.py:279
  103.2 1.9 %collective-permute-start.5 = (bf16[1,64,24,256]{3,2,1,0:T(8,128)(2,1)S(1)}, bf16[1,64,24,256]{3,2,1,0:T(8,128)(2,1)S(1)}, u32[]{:S(2)}, u32[]{:S(2)}) collective-permute-start(bf16[1,64,24,256]{3,2,1,0:T(8,128)(2,1)S(1)} %get-tuple-element.15), channel_id=1, source_target_pairs={{4,0},{8,4},{12,8},{16,12},{20,16},{24,20},{28,24},{32,28},{36,32}... | collective-permute-start | bytes 2359304 | tf_op jit(solution)/shard_map/ppermute | solution.py:279
  105.1 12.8 %collective-permute-done.4 = bf16[1,64,24,256]{3,2,1,0:T(8,128)(2,1)S(1)} collective-permute-done((bf16[1,64,24,256]{3,2,1,0:T(8,128)(2,1)S(1)}, bf16[1,64,24,256]{3,2,1,0:T(8,128)(2,1)S(1)}, u32[]{:S(2)}, u32[]{:S(2)}) %collective-permute-start.4) | collective-permute-done | bytes 786464 | tf_op jit(solution)/shard_map/ppermute | solution.py:279
  117.9 7.7 %collective-permute-done.5 = bf16[1,64,24,256]{3,2,1,0:T(8,128)(2,1)S(1)} collective-permute-done((bf16[1,64,24,256]{3,2,1,0:T(8,128)(2,1)S(1)}, bf16[1,64,24,256]{3,2,1,0:T(8,128)(2,1)S(1)}, u32[]{:S(2)}, u32[]{:S(2)}) %collective-permute-start.5) | collective-permute-done | bytes 786464 | tf_op jit(solution)/shard_map/ppermute | solution.py:279
  125.6 0.0 copy-done.2
  125.6 2.8 %pad_maximum_fusion.brick = bf16[4,64,24,256]{3,2,1,0:T(8,128)(2,1)} fusion(bf16[1,64,24,256]{3,2,1,0:T(8,128)(2,1)S(1)} %collective-permute-done.5, bf16[2,64,6,256]{3,2,1,0:T(8,128)(2,1)S(1)} %broadcast_in_dim.137, bf16[2,64,1,256]{3,2,1,0:T(2,128)(2,1)S(1)} %collective-permute-done.3, bf16[2,64,16,256]{3,2,1,0:T(8,128)(2,1)S(1)} %copy-done.2, ...), kind=kLoop, calls=%fused_computation.11 | loop fusion | flops 18874368 | bytes 6291456 | tf_op jit(solution)/shard_map/concatenate | solution.py:303
  128.4 13.9 %cube.3 = bf16[2,64,16,256]{3,2,1,0:T(8,128)(2,1)} custom-call(bf16[4,64,24,256]{3,2,1,0:T(8,128)(2,1)} %pad_maximum_fusion.brick, bf16[6912,256]{1,0:T(8,128)(2,1)} %bitcast.24, f32[1,256]{1,0:T(1,128)} %bitcast.39), custom_call_target="tpu_custom_call" | custom-call | tf_op jit(solution)/shard_map/cube/pallas_call | solution.py:263
  142.3 3.3 %copy.12 = bf16[64,16,2,256]{3,2,1,0:T(2,128)(2,1)} copy(bf16[64,16,2,256]{3,1,0,2:T(8,128)(2,1)} %bitcast.23) | data formatting | bytes 2097152 | tf_op jit(solution)/shard_map/transpose | solution.py:304
  (19 shorter events, 0.2 us)
Async XLA Ops:
  0.8 14.3 %collective-permute-start = (bf16[2,16,512]{2,1,0:T(8,128)(2,1)S(1)}, bf16[2,16,512]{2,1,0:T(8,128)(2,1)S(1)}, u32[]{:S(2)}, u32[]{:S(2)}) collective-permute-start(bf16[2,16,512]{2,1,0:T(8,128)(2,1)S(1)} %get-tuple-element.18), channel_id=1, source_target_pairs={{0,1},{1,2},{2,3},{4,5},{5,6},{6,7},{8,9},{9,10},{10,11},{12,13},{... | collective-permute-start | bytes 98312 | tf_op jit(solution)/shard_map/ppermute | solution.py:279
  4.9 10.2 %collective-permute-start.1 = (bf16[2,16,512]{2,1,0:T(8,128)(2,1)S(1)}, bf16[2,16,512]{2,1,0:T(8,128)(2,1)S(1)}, u32[]{:S(2)}, u32[]{:S(2)}) collective-permute-start(bf16[2,16,512]{2,1,0:T(8,128)(2,1)S(1)} %get-tuple-element.19), channel_id=1, source_target_pairs={{1,0},{2,1},{3,2},{5,4},{6,5},{7,6},{9,8},{10,9},{11,10},{13,12},{... | collective-permute-start | bytes 98312 | tf_op jit(solution)/shard_map/ppermute | solution.py:279
  10.1 3.0 %copy-start.4 = (f32[32]{0:T(128)S(1)}, f32[32]{0:T(128)}, u32[]{:S(2)}) copy-start(f32[32]{0:T(128)} %param.13) | copy-start | bytes 388
  10.1 3.1 %copy-start.5 = (f32[64]{0:T(128)S(1)}, f32[64]{0:T(128)}, u32[]{:S(2)}) copy-start(f32[64]{0:T(128)} %param.15) | copy-start | bytes 772
  12.9 2.2 %copy-start.3 = (bf16[2,128,512]{2,1,0:T(8,128)(2,1)S(1)}, bf16[2,128,512]{2,1,0:T(8,128)(2,1)}, u32[]{:S(2)}) copy-start(bf16[2,128,512]{2,1,0:T(8,128)(2,1)} %param.11) | copy-start | bytes 786436
  12.9 2.4 %copy-start.1 = (f32[128]{0:T(128)S(1)}, f32[128]{0:T(128)}, u32[]{:S(2)}) copy-start(f32[128]{0:T(128)} %param.17) | copy-start | bytes 1540
  43.5 0.9 copy-start
  84.8 5.2 %collective-permute-start.2 = (bf16[2,64,1,256]{3,2,1,0:T(2,128)(2,1)S(1)}, bf16[2,64,1,256]{3,2,1,0:T(2,128)(2,1)S(1)}, u32[]{:S(2)}, u32[]{:S(2)}) collective-permute-start(bf16[2,64,1,256]{3,2,1,0:T(2,128)(2,1)S(1)} %get-tuple-element.16), channel_id=1, source_target_pairs={{0,1},{1,2},{2,3},{4,5},{5,6},{6,7},{8,9},{9,10},{10,11},{12,13},{... | collective-permute-start | bytes 196616 | tf_op jit(solution)/shard_map/ppermute | solution.py:279
  88.2 6.3 %collective-permute-start.3 = (bf16[2,64,1,256]{3,2,1,0:T(2,128)(2,1)S(1)}, bf16[2,64,1,256]{3,2,1,0:T(2,128)(2,1)S(1)}, u32[]{:S(2)}, u32[]{:S(2)}) collective-permute-start(bf16[2,64,1,256]{3,2,1,0:T(2,128)(2,1)S(1)} %get-tuple-element.17), channel_id=1, source_target_pairs={{1,0},{2,1},{3,2},{5,4},{6,5},{7,6},{9,8},{10,9},{11,10},{13,12},{... | collective-permute-start | bytes 196616 | tf_op jit(solution)/shard_map/ppermute | solution.py:279
  94.5 31.2 %copy-start.2 = (bf16[2,64,16,256]{3,2,1,0:T(8,128)(2,1)S(1)}, bf16[2,64,16,256]{3,2,1,0:T(8,128)(2,1)}, u32[]{:S(2)}) copy-start(bf16[2,64,16,256]{3,2,1,0:T(8,128)(2,1)} %cube.2) | copy-start | bytes 3145732
  97.3 20.6 %collective-permute-start.4 = (bf16[1,64,24,256]{3,2,1,0:T(8,128)(2,1)S(1)}, bf16[1,64,24,256]{3,2,1,0:T(8,128)(2,1)S(1)}, u32[]{:S(2)}, u32[]{:S(2)}) collective-permute-start(bf16[1,64,24,256]{3,2,1,0:T(8,128)(2,1)S(1)} %get-tuple-element.14), channel_id=1, source_target_pairs={{0,4},{4,8},{8,12},{12,16},{16,20},{20,24},{24,28},{28,32},{32,36}... | collective-permute-start | bytes 2359304 | tf_op jit(solution)/shard_map/ppermute | solution.py:279
  103.2 22.5 %collective-permute-start.5 = (bf16[1,64,24,256]{3,2,1,0:T(8,128)(2,1)S(1)}, bf16[1,64,24,256]{3,2,1,0:T(8,128)(2,1)S(1)}, u32[]{:S(2)}, u32[]{:S(2)}) collective-permute-start(bf16[1,64,24,256]{3,2,1,0:T(8,128)(2,1)S(1)} %get-tuple-element.15), channel_id=1, source_target_pairs={{4,0},{8,4},{12,8},{16,12},{20,16},{24,20},{28,24},{32,28},{36,32}... | collective-permute-start | bytes 2359304 | tf_op jit(solution)/shard_map/ppermute | solution.py:279
where the time goes:
time: 146 us
  Pallas kernels  81.1 us (56%)
  waiting for transfers between devices  24.9 us (17%)
  starting transfers between devices  19 us (13%)
  local copies, waits for them, and re-layouts  11.6 us (8%)
  other arithmetic  8.62 us (6%)
    pallas_call x1, Pallas kernels, turn(): pl.pallas_call(functools.partial(turn_kernel, peers), name='turn', out_sh...  29.8 us
    pallas_call x1, Pallas kernels, plane_levels(): pl.pallas_call(plane_kernel, name='plane_levels', out_shape=jax.ShapeDtyp...  28.2 us
    ppermute x6, waiting for transfers between devices, shift(): return lax.ppermute(block, axis, pairs)  24.9 us
    pallas_call x2, Pallas kernels, cube(): pl.pallas_call(functools.partial(cube_kernel, depth, chans), name='cube',...  23.2 us
    ppermute x6, starting transfers between devices, shift(): return lax.ppermute(block, axis, pairs)  19 us
    transpose x1, local copies, waits for them, and re-layouts, body(): return jnp.transpose(out, (1, 2, 0, 3))  3.27 us
  transfers between devices with their start and end apart: 6, of which 3 were waited for; matrix products, arithmetic and copies ran while one was open for 6% of the time, Pallas kernels for 0%

commit v1 on v0

v1 whole, which is shorter than its diff:
```python
import functools

import jax
import jax.numpy as jnp
from jax import lax
from jax.experimental import pallas as pl
from jax.experimental.pallas import tpu as pltpu
from jax.sharding import PartitionSpec as P

F32 = jnp.float32
BF16 = jnp.bfloat16
MESH = pl.DeviceIdType.MESH
VMEM = pl.BlockSpec(memory_space=pltpu.VMEM)
ANY = pl.BlockSpec(memory_space=pl.ANY)
ROWS = 168
WINS = 10
CHUNKS = ((0, 4, 0, 7), (4, 7, 7, 13), (7, 10, 13, 19))


def picker():
    source = lax.broadcasted_iota(jnp.int32, (512, 1280), 0)
    column = lax.broadcasted_iota(jnp.int32, (512, 1280), 1)
    j, m = column // 128, column % 128
    x2 = 2 * (m % 64) + m // 64
    return (source == 4 * x2 - 3 + j).astype(BF16)


def banded_first(weight):
    taps = jnp.tile(jnp.transpose(weight[:, 0], (1, 2, 0)), (1, 1, 8))
    lane = lax.broadcasted_iota(jnp.int32, (10, 256), 1)
    j = lax.broadcasted_iota(jnp.int32, (10, 256), 0)
    first = 2 * ((lane // 32) % 4) + lane // 128
    rows = lax.broadcasted_iota(jnp.int32, (16, 10, 24, 256), 2)
    step = lax.broadcasted_iota(jnp.int32, (16, 10, 24, 256), 0)
    total = jnp.zeros((16, 10, 24, 256), BF16)
    for ky in range(3):
        cols = jnp.zeros((10, 256), BF16)
        for kx in range(3):
            cols = jnp.where(j == first + kx, taps[ky, kx][None, :], cols)
        total = jnp.where(rows == step + 1 + ky, cols[None, :, None, :], total)
    return jnp.pad(total.reshape(16, 240, 256), ((0, 0), (0, 16), (0, 0)))


def banded_second(weight):
    taps = jnp.transpose(weight, (2, 3, 1, 0))
    parts = [
        jnp.pad(taps, ((py, 1 - py), (px, 1 - px), (0, 0), (0, 0))).reshape(512, 64)
        for py in range(2)
        for px in range(2)
    ]
    return jnp.concatenate(parts, axis=1)


def banded_third(weight):
    taps = jnp.transpose(weight, (2, 3, 1, 0))
    parts = [jnp.pad(taps, ((0, 0), (px, 1 - px), (0, 0), (0, 0))).reshape(768, 128) for px in range(2)]
    return jnp.concatenate(parts, axis=1)


def shifted(rows):
    sub = lax.broadcasted_iota(jnp.int32, rows.shape, 0)
    last = rows.shape[0] - 1
    down = jnp.where(sub == 0, 0.0, pltpu.roll(rows, 1, 0))
    up = jnp.where(sub == last, 0.0, pltpu.roll(rows, last, 0))
    return down, up


def kernel(
    nx, ny, raw, pick, w1, b1, w2, b2, w3, b3, wa_hbm, ba, wb_hbm, bb,
    out,
    padded, spread, turned, first, second, third, slab, brick, tall, mid, wa, wb,
    raw_send, raw_recv, turn_send, turn_recv, own_sem, load_sem,
    side_send, side_recv, edge_send, edge_recv, corner_send, corner_recv,
):
    me = lax.axis_index("gz")
    yi = lax.axis_index("xy")
    has = {-1: yi > 0, 1: yi < ny - 1}
    hasx = {-1: me > 0, 1: me < nx - 1}

    load_a = pltpu.make_async_copy(wa_hbm, wa, load_sem.at[0])
    load_b = pltpu.make_async_copy(wb_hbm, wb, load_sem.at[1])
    load_a.start()
    load_b.start()

    barrier = pltpu.get_barrier_semaphore()

    def greet(gx, gy):
        pl.semaphore_signal(barrier, inc=1, device_id=(gx, gy), device_id_type=MESH)

    @pl.loop(1, nx)
    def _(k):
        greet(lax.rem(me + k, nx), yi)

    for dy in (-1, 1):

        @pl.when(has[dy])
        def _():
            greet(me, yi + dy)

        for dx in (-1, 1):

            @pl.when(jnp.logical_and(has[dy], hasx[dx]))
            def _():
                greet(me + dx, yi + dy)

    one = lambda flag: jnp.where(flag, 1, 0)
    tall_n = one(has[-1]) + one(has[1])
    wide_n = one(hasx[-1]) + one(hasx[1])
    pl.semaphore_wait(barrier, nx - 1 + tall_n + tall_n * wide_n)

    def raw_copy(dy):
        k = (dy + 1) // 2
        src = raw.at[:, pl.ds(112 if dy == 1 else 0, 16)]
        dst = padded.at[:, pl.ds(0 if dy == 1 else 144, 16)]
        return pltpu.make_async_remote_copy(
            src_ref=src, dst_ref=dst, send_sem=raw_send.at[k], recv_sem=raw_recv.at[k],
            device_id=(me, yi + dy), device_id_type=MESH,
        )

    for dy in (-1, 1):

        @pl.when(has[dy])
        def _():
            raw_copy(dy).start()

        @pl.when(jnp.logical_not(has[dy]))
        def _():
            padded[:, pl.ds(0 if dy == -1 else 144, 16)] = jnp.zeros((2, 16, 512), BF16)

    padded[:, pl.ds(16, 128)] = raw[...]
    padded[:, pl.ds(160, 8)] = jnp.zeros((2, 8, 512), BF16)
    for dx in (-1, 1):

        @pl.when(jnp.logical_not(hasx[dx]))
        def _():
            col = 0 if dx == -1 else 3

            @pl.loop(0, 18)
            def _(r):
                for kz in range(3):
                    mid[kz, col, r] = jnp.zeros((64, 256), BF16)

    for dy in (-1, 1):

        @pl.when(jnp.logical_not(has[dy]))
        def _():
            row = 0 if dy == -1 else 17
            for kz in range(3):
                for x in range(4):
                    mid[kz, x, row] = jnp.zeros((64, 256), BF16)

    for c in range(3):
        slab[c, 0] = jnp.zeros((2, 8, 128), BF16)
        slab[c, 65] = jnp.zeros((2, 8, 128), BF16)

    for dy in (-1, 1):

        @pl.when(has[dy])
        def _():
            raw_copy(dy).wait_send()

        @pl.when(has[-dy])
        def _():
            raw_copy(dy).wait_recv()

    lane = lax.broadcasted_iota(jnp.int32, (128, 128), 1)
    sub = lax.broadcasted_iota(jnp.int32, (128, 128), 0)
    outside = jnp.logical_or(
        jnp.logical_and(sub == 0, lane < 32), jnp.logical_and(sub == 127, lane >= 96)
    )
    inside_f = jnp.where(outside, 0.0, 1.0)
    lane64 = lax.broadcasted_iota(jnp.int32, (64, 128), 1)
    half = lane64 < 64

    def keep(place, size):
        return jnp.where(jnp.logical_and(place >= 0, place < size * ny), 1.0, 0.0)

    @pl.loop(0, 2)
    def _(z):
        spread[...] = jnp.dot(padded[z], pick[...], preferred_element_type=F32)

        @pl.loop(0, WINS)
        def _(w):
            rows = pl.ds(pl.multiple_of(w * 16, 16), 24)
            parts = [spread[rows, j * 128 : (j + 1) * 128] for j in range(10)]
            parts.append(jnp.zeros((16, 128), F32))
            turned[w, z] = jnp.concatenate(parts, axis=0).T.astype(BF16)

    def turn_copy(c, k):
        there = lax.rem(me + k, nx)
        return pltpu.make_async_remote_copy(
            src_ref=slab.at[c, pl.ds(2 * there, 4)],
            dst_ref=brick.at[c, :, pl.ds(2 * me, 2)],
            send_sem=turn_send.at[c, k],
            recv_sem=turn_recv.at[c, k],
            device_id=(there, yi),
            device_id_type=MESH,
        )

    def own_copy(c):
        return pltpu.make_async_copy(
            slab.at[c, pl.ds(2 * me, 4)], brick.at[c, :, pl.ds(2 * me, 2)], own_sem.at[c]
        )

    for c, (w_begin, w_end, p_begin, p_end) in enumerate(CHUNKS):

        @pl.loop(0, 8)
        def _(i):
            for w in range(w_begin, w_end):
                lhs = turned[w].reshape(256, 256)
                top = jnp.maximum(
                    jnp.dot(lhs, w1[2 * i], preferred_element_type=F32),
                    jnp.dot(lhs, w1[2 * i + 1], preferred_element_type=F32),
                )
                top = jnp.maximum(top[:, :128], top[:, 128:])
                top = jnp.maximum(top + b1[...], 0.0).reshape(2, 128, 128)
                row = 8 * w + i
                scale = inside_f * keep(64 * yi + row - 7, 64)
                for z in range(2):
                    first[z, row] = (top[z] * scale).astype(BF16)

        @pl.loop(p_begin, p_end)
        def _(g):
            base = 4 * g
            lhs = jnp.concatenate(
                [
                    jnp.concatenate([first[z, base + 2 * k + a] for a in range(4)], axis=1)
                    for z in range(2)
                    for k in range(2)
                ],
                axis=0,
            )
            res = jnp.dot(lhs, w2[...], preferred_element_type=F32)
            top = jnp.maximum(res[:, :128], res[:, 128:])
            top = jnp.maximum(top, pltpu.roll(top, 64, 1))
            top = jnp.maximum(top + b2[...], 0.0).reshape(2, 2, 128, 128)
            for k in range(2):
                q = 2 * g + k
                scale = keep(32 * yi + q - 3, 32)
                for z in range(2):
                    val = top[z, k] * scale
                    even, odd = val[:64], val[64:]
                    down = shifted(odd)[0]
                    up = shifted(even)[1]
                    second[z, q, :, :128] = jnp.where(half, down, even).astype(BF16)
                    second[z, q, :, 128:] = jnp.where(half, odd, up).astype(BF16)

        @pl.loop(3 * c, 3 * c + 3)
        def _(g):
            base = 4 * g
            lhs = jnp.concatenate(
                [
                    jnp.concatenate(
                        [second[z, pl.ds(base + ky, 4)].reshape(256, 256) for ky in range(3)], axis=1
                    )
                    for z in range(2)
                ],
                axis=0,
            )
            res = jnp.dot(lhs, w3[...], preferred_element_type=F32)
            top = jnp.maximum(res[:, :128], res[:, 128:]).reshape(2, 2, 2, 64, 128)
            top = jnp.maximum(top[:, :, 0], top[:, :, 1])
            top = jnp.maximum(top + b3[...], 0.0)
            for k in range(2):
                t = 2 * g + k
                scale = keep(16 * yi + t - 1, 16)
                for z in range(2):
                    third[z, t - 6 * c] = top[z, k] * scale

        for z in range(2):
            for r in range(6, 8):
                third[z, r] = jnp.zeros((64, 128), F32)

            @pl.loop(0, 8)
            def _(g):
                x0 = pl.multiple_of(8 * g, 8)
                block = third[z, :, pl.ds(x0, 8), :]
                slab[c, pl.ds(1 + x0, 8), z] = jnp.transpose(block, (1, 0, 2)).astype(BF16)

        own_copy(c).start()

        @pl.loop(1, nx)
        def _(k):
            turn_copy(c, k).start()

    def side_copy(dx, g):
        k = (dx + 1) // 2
        rows = pl.ds(1 + 2 * g, 2)
        return pltpu.make_async_remote_copy(
            src_ref=mid.at[1, 1 if dx == -1 else 2, rows],
            dst_ref=mid.at[1, 3 if dx == -1 else 0, rows],
            send_sem=side_send.at[k, g], recv_sem=side_recv.at[k, g],
            device_id=(me + dx, yi), device_id_type=MESH,
        )

    def edge_copy(dy):
        k = (dy + 1) // 2
        return pltpu.make_async_remote_copy(
            src_ref=mid.at[1, pl.ds(1, 2), 1 if dy == -1 else 16],
            dst_ref=mid.at[1, pl.ds(1, 2), 17 if dy == -1 else 0],
            send_sem=edge_send.at[k], recv_sem=edge_recv.at[k],
            device_id=(me, yi + dy), device_id_type=MESH,
        )

    def corner_copy(dx, dy):
        k, j = (dx + 1) // 2, (dy + 1) // 2
        return pltpu.make_async_remote_copy(
            src_ref=mid.at[1, 1 if dx == -1 else 2, 1 if dy == -1 else 16],
            dst_ref=mid.at[1, 3 if dx == -1 else 0, 17 if dy == -1 else 0],
            send_sem=corner_send.at[k, j], recv_sem=corner_recv.at[k, j],
            device_id=(me + dx, yi + dy), device_id_type=MESH,
        )

    def send_sides(g):
        for dx in (-1, 1):

            @pl.when(hasx[dx])
            def _():
                side_copy(dx, g).start()

    def send_edges(dy):
        @pl.when(has[dy])
        def _():
            edge_copy(dy).start()

        for dx in (-1, 1):

            @pl.when(jnp.logical_and(has[dy], hasx[dx]))
            def _():
                corner_copy(dx, dy).start()

    def cube_rows(source, weight, g, chans):
        lhs = jnp.concatenate(
            [
                jnp.concatenate(
                    [
                        source[kz, x + kx, pl.ds(2 * g + ky, 2)].reshape(128, chans)
                        for kz in range(3)
                        for ky in range(3)
                        for kx in range(3)
                    ],
                    axis=1,
                )
                for x in range(2)
            ],
            axis=0,
        )
        return jnp.dot(lhs, weight[...], preferred_element_type=F32)

    load_a.wait()
    for c, (g_begin, g_end) in enumerate(((0, 2), (2, 5), (5, 8))):
        own_copy(c).wait()

        @pl.loop(1, nx)
        def _(k):
            turn_copy(c, k).wait_recv()

        @pl.loop(0, 4)
        def _(x):
            rows = jnp.transpose(brick[c, x].astype(F32), (1, 0, 2))
            for r in range(6):
                down, up = shifted(rows[r])
                tall[0, x, 6 * c + r] = down.astype(BF16)
                tall[1, x, 6 * c + r] = rows[r].astype(BF16)
                tall[2, x, 6 * c + r] = up.astype(BF16)

        @pl.loop(g_begin, g_end)
        def _(g):
            res = cube_rows(tall, wa, g, 128)
            res = jnp.maximum(res + ba[...], 0.0).reshape(2, 2, 64, 256)
            for x in range(2):
                for r in range(2):
                    down, up = shifted(res[x, r])
                    mid[0, 1 + x, 1 + 2 * g + r] = down.astype(BF16)
                    mid[1, 1 + x, 1 + 2 * g + r] = res[x, r].astype(BF16)
                    mid[2, 1 + x, 1 + 2 * g + r] = up.astype(BF16)
            send_sides(g)

        if c == 0:
            send_edges(-1)
        if c == 2:
            send_edges(1)

    def spread_row(x, r):
        down, up = shifted(mid[1, x, r].astype(F32))
        mid[0, x, r] = down.astype(BF16)
        mid[2, x, r] = up.astype(BF16)

    def take_sides(g):
        for dx in (-1, 1):

            @pl.when(hasx[-dx])
            def _():
                side_copy(dx, g).wait_recv()
                for r in range(2):
                    spread_row(3 if dx == -1 else 0, 1 + 2 * g + r)

    def take_edges(dy):
        row = 17 if dy == -1 else 0

        @pl.when(has[-dy])
        def _():
            edge_copy(dy).wait_recv()
            spread_row(1, row)
            spread_row(2, row)

        for dx in (-1, 1):

            @pl.when(jnp.logical_and(has[-dy], hasx[-dx]))
            def _():
                corner_copy(dx, dy).wait_recv()
                spread_row(3 if dx == -1 else 0, row)

    def last_rows(g):
        res = cube_rows(mid, wb, g, 256)
        res = jnp.maximum(res + bb[...], 0.0).astype(BF16).reshape(2, 2, 64, 256)
        for x in range(2):
            for r in range(2):
                out[x, 2 * g + r] = res[x, r]

    load_b.wait()
    take_sides(0)
    take_sides(1)

    @pl.loop(1, 7)
    def _(g):
        take_sides(g + 1)
        last_rows(g)

    take_edges(-1)
    last_rows(7)
    take_edges(1)
    last_rows(0)

    for c in range(3):

        @pl.loop(1, nx)
        def _(k):
            turn_copy(c, k).wait_send()

    for dx in (-1, 1):

        @pl.when(hasx[dx])
        def _():
            @pl.loop(0, 8)
            def _(g):
                side_copy(dx, g).wait_send()

    for dy in (-1, 1):

        @pl.when(has[dy])
        def _():
            edge_copy(dy).wait_send()

        for dx in (-1, 1):

            @pl.when(jnp.logical_and(has[dy], hasx[dx]))
            def _():
                corner_copy(dx, dy).wait_send()


def body(raw, wf, bf, ws, bs, wt, bt, wa, ba, wb, bb):
    nx, ny = lax.axis_size("gz"), lax.axis_size("xy")
    dma = pltpu.SemaphoreType.DMA
    out = pl.pallas_call(
        functools.partial(kernel, nx, ny),
        name="encoder",
        out_shape=jax.ShapeDtypeStruct((2, 16, 64, 256), BF16),
        in_specs=[VMEM] * 8 + [ANY, VMEM, ANY, VMEM],
        out_specs=VMEM,
        scratch_shapes=[
            pltpu.VMEM((2, ROWS, 512), BF16),
            pltpu.VMEM((ROWS, 1280), F32),
            pltpu.VMEM((WINS, 2, 128, 256), BF16),
            pltpu.VMEM((2, 80, 128, 128), BF16),
            pltpu.VMEM((2, 38, 64, 256), BF16),
            pltpu.VMEM((2, 8, 64, 128), F32),
            pltpu.VMEM((3, 66, 2, 8, 128), BF16),
            pltpu.VMEM((3, 4, 64, 8, 128), BF16),
            pltpu.VMEM((3, 4, 18, 64, 128), BF16),
            pltpu.VMEM((3, 4, 18, 64, 256), BF16),
            pltpu.VMEM((27 * 128, 256), BF16),
            pltpu.VMEM((27 * 256, 256), BF16),
            dma((2,)), dma((2,)), dma((3, nx)), dma((3, nx)), dma((3,)), dma((2,)),
            dma((2, 8)), dma((2, 8)), dma((2,)), dma((2,)), dma((2, 2)), dma((2, 2)),
        ],
        compiler_params=pltpu.CompilerParams(
            collective_id=0, has_side_effects=True, vmem_limit_bytes=60 << 20
        ),
    )(
        raw,
        picker(),
        banded_first(wf),
        jnp.tile(bf, 4).reshape(1, 128),
        banded_second(ws),
        jnp.tile(bs, 2).reshape(1, 128),
        banded_third(wt),
        bt.reshape(1, 128),
        wa.reshape(27 * 128, 256),
        ba.reshape(1, 256),
        wb.reshape(27 * 256, 256),
        bb.reshape(1, 256),
    )
    return jnp.transpose(out, (2, 1, 0, 3))


def solution(mesh):
    placed = (P("gz", "xy", None), P(), P(), P(), P(), P(), P(), P(), P(), P(), P())
    return jax.shard_map(
        body, mesh=mesh, in_specs=placed, out_specs=P(None, "xy", "gz", None), check_vma=False
    )
```

time: 146 us -> 85.3 us (0.58)
  the two profiles are of different devices: /device:TPU:31 before, /device:TPU:25 now
where the time goes in v1:
time: 85.3 us; the launch traced here: 85.1 us
  Pallas kernels  73.6 us (86%)
  local copies, waits for them, and re-layouts  7.19 us (8%)
  other arithmetic  4.19 us (5%)
    pallas_call x1, Pallas kernels, body(): pl.pallas_call(functools.partial(kernel, nx, ny), name='encoder', out_sha...  73.6 us
    transpose x1, local copies, waits for them, and re-layouts, body(): return jnp.transpose(out, (2, 1, 0, 3))  3.28 us

profile of v1, /device:TPU:25, one launch (start us, length us, event | category | flops | bytes accessed | tf_op | source)
XLA Modules:
  0.0 85.1 jit_solution(3456755260203557924)
XLA Ops:
  0.0 0.7 tile.8
  0.7 0.1 tile.9
  1.0 0.1 iota.226
  1.1 0.0 copy-start.1
  1.1 1.0 %compare_select_fusion.2 = bf16[16,240,256]{2,1,0:T(8,128)(2,1)S(1)} fusion(s32[16]{0:T(128)S(1)} %get-tuple-element.35, s32[16]{0:T(128)S(1)} %get-tuple-element.36, s32[16]{0:T(128)S(1)} %iota_add_fusion.2, s32[240]{0:T(256)S(1)} %iota.226, bf16[240,256]{1,0:T(8,128)(2,1)S(1)} %bitcast.33, bf16[240,256]{1,0:T(8,128)(2,1)S(1)} %bitcast.32, ...), kind=kLoop, calls=%fused_computation.10 | loop fusion | flops 5898240 | bytes 2335872 | tf_op jit(solution)/shard_map/jit(_where)/select_n | solution.py:40
  2.1 0.0 copy-start
  2.1 1.6 %pad.28.w1 = bf16[16,256,256]{2,1,0:T(8,128)(2,1)} pad(bf16[16,240,256]{2,1,0:T(8,128)(2,1)S(1)} %compare_select_fusion.2, bf16[]{:T(256)} %constant.107.clone.1), padding=0_0x0_16x0_0 | pad | bytes 4063234 | tf_op jit(solution)/shard_map/jit(_pad)/pad | solution.py:41
  3.7 0.0 copy-start.2
  3.7 0.0 copy-start.3
  3.7 0.0 copy-done.1
  3.7 0.1 fusion.22
  3.8 0.9 %pad_maximum_fusion.1.w2 = bf16[512,256]{1,0:T(8,128)(2,1)} fusion(bf16[512,64]{1,0:T(8,128)(2,1)S(1)} %bitcast.28, bf16[512,64]{1,0:T(8,128)(2,1)S(1)} %bitcast.29, bf16[512,64]{1,0:T(8,128)(2,1)S(1)} %bitcast.30, bf16[512,64]{1,0:T(8,128)(2,1)S(1)} %bitcast.27), kind=kLoop, calls=%fused_computation.23 | loop fusion | flops 1048576 | bytes 524288 | tf_op jit(solution)/shard_map/concatenate | solution.py:51
  4.7 1.4 %fusion.10.pick = bf16[512,1280]{1,0:T(8,128)(2,1)} fusion(s32[1280]{0:T(1024)S(1)} %get-tuple-element.23, s32[1280]{0:T(1024)S(1)} %get-tuple-element.26, s32[1280]{0:T(1024)S(1)} %get-tuple-element.24, s32[1280]{0:T(1024)S(1)} %get-tuple-element.25, pred[1280]{0:T(1024)(128)(4,1)S(1)} %get-tuple-element.27, pred[1280]{0:T(1024)(128)(4,1)S(1)} %get-tuple-element.28), kind=kLoop, calls=%fused_computation.21 | loop fusion | flops 18350080 | bytes 1333760 | tf_op jit(solution)/shard_map/convert_element_type | solution.py:25
  6.1 0.0 copy-done
  6.1 0.1 fusion.21
  6.2 0.8 pad_maximum_fusion.w3
  7.0 0.0 copy-done.2
  7.0 0.6 reshape_tile.6.b1
  7.6 0.0 copy-done.3
  7.6 0.7 reshape_tile.7.b2
  8.2 73.6 %encoder.1 = bf16[2,16,64,256]{3,2,1,0:T(8,128)(2,1)} custom-call(bf16[2,128,512]{2,1,0:T(8,128)(2,1)} %raw.1, bf16[512,1280]{1,0:T(8,128)(2,1)} %fusion.10.pick, bf16[16,256,256]{2,1,0:T(8,128)(2,1)} %pad.28.w1, f32[1,128]{1,0:T(1,128)} %reshape_tile.6.b1, bf16[512,256]{1,0:T(8,128)(2,1)} %pad_maximum_fusion.1.w2, f32[1,128]{1,0:T(1,128)} %reshape_tile.7.b2, ...), custom_call_target="tpu_custom_call" | custom-call | tf_op jit(solution)/shard_map/encoder/pallas_call | solution.py:465
  81.8 3.3 %copy.12 = bf16[64,16,2,256]{3,2,1,0:T(2,128)(2,1)} copy(bf16[64,16,2,256]{3,0,1,2:T(8,128)(2,1)} %bitcast.22) | data formatting | bytes 2097152 | tf_op jit(solution)/shard_map/transpose | solution.py:504
  (16 shorter events, 0.2 us)
Async XLA Ops:
  1.1 2.6 %copy-start.1 = (bf16[64,32,3,3]{0,1,3,2:T(8,128)(2,1)S(1)}, bf16[64,32,3,3]{0,1,3,2:T(8,128)(2,1)}, u32[]{:S(2)}) copy-start(bf16[64,32,3,3]{0,1,3,2:T(8,128)(2,1)} %param.14) | copy-start | bytes 110596
  2.1 4.0 %copy-start = (bf16[128,64,3,3]{0,1,3,2:T(8,128)(2,1)S(1)}, bf16[128,64,3,3]{0,1,3,2:T(8,128)(2,1)}, u32[]{:S(2)}) copy-start(bf16[128,64,3,3]{0,1,3,2:T(8,128)(2,1)} %param.16) | copy-start | bytes 442372
  3.7 3.3 %copy-start.2 = (f32[32]{0:T(128)S(1)}, f32[32]{0:T(128)}, u32[]{:S(2)}) copy-start(f32[32]{0:T(128)} %param.13) | copy-start | bytes 388
  3.7 3.9 %copy-start.3 = (f32[64]{0:T(128)S(1)}, f32[64]{0:T(128)}, u32[]{:S(2)}) copy-start(f32[64]{0:T(128)} %param.15) | copy-start | bytes 772

commit v2 on v1

v2 whole, which is shorter than its diff:
```python
import functools

import jax
import jax.numpy as jnp
from jax import lax
from jax.experimental import pallas as pl
from jax.experimental.pallas import tpu as pltpu
from jax.sharding import PartitionSpec as P

F32 = jnp.float32
BF16 = jnp.bfloat16
MESH = pl.DeviceIdType.MESH
VMEM = pl.BlockSpec(memory_space=pltpu.VMEM)
ANY = pl.BlockSpec(memory_space=pl.ANY)
ROWS = 168
WINS = 5
CHUNKS = (((0, 2), (0, 14), (0, 6)), ((2, 4), (14, 30), (6, 14)), ((4, 5), (30, 38), (14, 18)))
TILE = (8, 8, 4)


def banded_second(weight):
    taps = jnp.transpose(weight, (2, 3, 1, 0))
    parts = [
        jnp.pad(taps, ((py, 1 - py), (px, 1 - px), (0, 0), (0, 0))).reshape(512, 64)
        for py in range(2)
        for px in range(2)
    ]
    return jnp.concatenate(parts, axis=1)


def banded_third(weight):
    taps = jnp.transpose(weight, (2, 3, 1, 0))
    parts = [jnp.pad(taps, ((0, 0), (px, 1 - px), (0, 0), (0, 0))).reshape(768, 128) for px in range(2)]
    return jnp.concatenate(parts, axis=1)


def shifted(rows):
    sub = lax.broadcasted_iota(jnp.int32, rows.shape, 0)
    last = rows.shape[0] - 1
    down = jnp.where(sub == 0, 0.0, pltpu.roll(rows, 1, 0))
    up = jnp.where(sub == last, 0.0, pltpu.roll(rows, last, 0))
    return down, up


def make_pick(pick):
    source = lax.broadcasted_iota(jnp.int32, (512, 128), 0)
    m = lax.broadcasted_iota(jnp.int32, (512, 128), 1)
    start = 8 * jnp.where(m < 64, m, m - 64) + jnp.where(m < 64, 0, 4) - 1
    gap = source - start
    for j in range(6):
        pick[:, 128 * j : 128 * j + 128] = jnp.where(gap == j, 1.0, 0.0).astype(BF16)


def make_first(small, w1):
    lane = lax.broadcasted_iota(jnp.int32, (1, 256), 1)
    bit = lambda n: jnp.where(jnp.bitwise_and(lane, n) == 0, 0, 1)
    start = 2 * (1 - bit(32)) + bit(64)
    cols = []
    for j in range(6):
        for ky in range(3):
            total = jnp.zeros((1, 256), F32)
            for kx in range(3):
                total = jnp.where(start == j - kx, small[3 * ky + kx : 3 * ky + kx + 1, :], total)
            cols.append(jnp.broadcast_to(total, (40, 256)))
    wide = lax.broadcasted_iota(jnp.int32, (40, 256), 1)
    gap = lax.broadcasted_iota(jnp.int32, (40, 256), 0) - jnp.where(wide < 128, 1, 2)

    @pl.loop(0, 16)
    def _(i):
        hit = [gap == 2 * i + ky for ky in range(3)]
        for j in range(6):
            total = jnp.zeros((40, 256), F32)
            for ky in range(3):
                total = jnp.where(hit[ky], cols[3 * j + ky], total)
            w1[i, 40 * j : 40 * j + 40] = total.astype(BF16)
        w1[i, 240:] = jnp.zeros((16, 256), BF16)


def kernel(
    nx, ny, raw, small, w2, w3, wa_hbm, wb_hbm,
    out,
    padded, pick, w1, spread, turned, first, second, third,
    slab_0, slab_1, slab_2, brick_0, brick_1, brick_2, tall, mid, wa, wb,
    raw_send, raw_recv, turn_send, turn_recv, own_sem, load_sem,
    side_send, side_recv, edge_send, edge_recv, corner_send, corner_recv,
):
    me = lax.axis_index("gz")
    yi = lax.axis_index("xy")
    slab, brick = (slab_0, slab_1, slab_2), (brick_0, brick_1, brick_2)
    has = {-1: yi > 0, 1: yi < ny - 1}
    hasx = {-1: me > 0, 1: me < nx - 1}

    load_a = pltpu.make_async_copy(wa_hbm, wa, load_sem.at[0])
    load_b = pltpu.make_async_copy(wb_hbm, wb, load_sem.at[1])
    load_a.start()
    load_b.start()

    barrier = pltpu.get_barrier_semaphore()

    def greet(gx, gy):
        pl.semaphore_signal(barrier, inc=1, device_id=(gx, gy), device_id_type=MESH)

    @pl.loop(1, nx)
    def _(k):
        greet(lax.rem(me + k, nx), yi)

    for dy in (-1, 1):

        @pl.when(has[dy])
        def _():
            greet(me, yi + dy)

        for dx in (-1, 1):

            @pl.when(jnp.logical_and(has[dy], hasx[dx]))
            def _():
                greet(me + dx, yi + dy)

    make_pick(pick)
    one = lambda flag: jnp.where(flag, 1, 0)
    tall_n = one(has[-1]) + one(has[1])
    wide_n = one(hasx[-1]) + one(hasx[1])
    pl.semaphore_wait(barrier, nx - 1 + tall_n + tall_n * wide_n)

    def raw_copy(dy):
        k = (dy + 1) // 2
        src = raw.at[:, pl.ds(112 if dy == 1 else 0, 16)]
        dst = padded.at[:, pl.ds(0 if dy == 1 else 144, 16)]
        return pltpu.make_async_remote_copy(
            src_ref=src, dst_ref=dst, send_sem=raw_send.at[k], recv_sem=raw_recv.at[k],
            device_id=(me, yi + dy), device_id_type=MESH,
        )

    for dy in (-1, 1):

        @pl.when(has[dy])
        def _():
            raw_copy(dy).start()

        @pl.when(jnp.logical_not(has[dy]))
        def _():
            padded[:, pl.ds(0 if dy == -1 else 144, 16)] = jnp.zeros((2, 16, 512), BF16)

    padded[:, pl.ds(16, 128)] = raw[...]
    padded[:, pl.ds(160, 8)] = jnp.zeros((2, 8, 512), BF16)
    for dx in (-1, 1):

        @pl.when(jnp.logical_not(hasx[dx]))
        def _():
            col = 0 if dx == -1 else 3

            @pl.loop(0, 18)
            def _(r):
                for kz in range(3):
                    mid[kz, col, r] = jnp.zeros((64, 256), BF16)

    for dy in (-1, 1):

        @pl.when(jnp.logical_not(has[dy]))
        def _():
            row = 0 if dy == -1 else 17
            for kz in range(3):
                for x in range(4):
                    mid[kz, x, row] = jnp.zeros((64, 256), BF16)

    for c in range(3):
        slab[c][0] = jnp.zeros((2, TILE[c], 128), BF16)
        slab[c][65] = jnp.zeros((2, TILE[c], 128), BF16)
    make_first(small, w1)

    for dy in (-1, 1):

        @pl.when(has[dy])
        def _():
            raw_copy(dy).wait_send()

        @pl.when(has[-dy])
        def _():
            raw_copy(dy).wait_recv()

    lane64 = lax.broadcasted_iota(jnp.int32, (64, 128), 1)
    low, high, half = lane64 < 32, lane64 >= 96, lane64 < 64
    b1, b2, b3 = small[9:10, :128], small[10:11, :128], small[11:12, :128]

    for z in range(2):
        spread[z] = jnp.dot(padded[z], pick[...], preferred_element_type=F32)
    for w in range(WINS):
        for z in range(2):
            parts = [spread[z, w * 32 : w * 32 + 40, j * 128 : (j + 1) * 128] for j in range(6)]
            parts.append(jnp.zeros((16, 128), F32))
            turned[w, z] = jnp.concatenate(parts, axis=0).T.astype(BF16)

    def turn_copy(c, k):
        there = lax.rem(me + k, nx)
        return pltpu.make_async_remote_copy(
            src_ref=slab[c].at[pl.ds(2 * there, 4)],
            dst_ref=brick[c].at[:, pl.ds(2 * me, 2)],
            send_sem=turn_send.at[c, k],
            recv_sem=turn_recv.at[c, k],
            device_id=(there, yi),
            device_id_type=MESH,
        )

    def own_copy(c):
        return pltpu.make_async_copy(
            slab[c].at[pl.ds(2 * me, 4)], brick[c].at[:, pl.ds(2 * me, 2)], own_sem.at[c]
        )

    def blank(ref, begin, end):
        for z in range(2):
            for r in range(begin, end):
                ref[z, r] = jnp.zeros(ref.shape[2:], ref.dtype)

    def outside(ref, c, above, below):
        if c == 0:
            pl.when(jnp.logical_not(has[-1]))(lambda: blank(ref, *above))
        if c == 2:
            pl.when(jnp.logical_not(has[1]))(lambda: blank(ref, *below))

    for c, ((w_begin, w_end), (q_begin, q_end), (t_begin, t_end)) in enumerate(CHUNKS):
        wins = w_end - w_begin
        for i in range(16):
            lhs = turned[w_begin:w_end].reshape(wins * 256, 256)
            res = jnp.dot(lhs, w1[i], preferred_element_type=F32)
            top = jnp.maximum(res[:, :128], res[:, 128:])
            top = jnp.maximum(top, pltpu.roll(top, 64, 1))
            top = jnp.maximum(top + b1, 0.0).reshape(wins, 2, 128, 128)
            for w in range(wins):
                for z in range(2):
                    even, odd = top[w, z, :64], top[w, z, 64:]
                    down, up = shifted(odd)[0], shifted(even)[1]
                    row = 16 * (w_begin + w) + i
                    left = jnp.where(low, down, jnp.where(high, odd, even))
                    right = jnp.where(low, even, jnp.where(high, up, odd))
                    first[z, row, :64] = left.astype(BF16)
                    first[z, row, 64:] = right.astype(BF16)
        outside(first, c, (0, 7), (71, 80))

        for q0 in range(q_begin, q_end, 2):
            lhs = jnp.concatenate(
                [
                    jnp.concatenate([first[z, 2 * (q0 + k) + a] for a in range(4)], axis=1)
                    for z in range(2)
                    for k in range(2)
                ],
                axis=0,
            )
            res = jnp.dot(lhs, w2[...], preferred_element_type=F32)
            top = jnp.maximum(res[:, :128], res[:, 128:])
            top = jnp.maximum(top, pltpu.roll(top, 64, 1))
            top = jnp.maximum(top + b2, 0.0).reshape(2, 2, 128, 128)
            for k in range(2):
                for z in range(2):
                    even, odd = top[z, k, :64], top[z, k, 64:]
                    down, up = shifted(odd)[0], shifted(even)[1]
                    second[z, q0 + k, :, :128] = jnp.where(half, down, even).astype(BF16)
                    second[z, q0 + k, :, 128:] = jnp.where(half, odd, up).astype(BF16)
        outside(second, c, (0, 3), (35, 38))

        nt = t_end - t_begin
        lhs = jnp.concatenate(
            [
                jnp.concatenate(
                    [
                        second[z, 2 * t_begin + ky : 2 * t_end + ky].reshape(nt * 128, 256)
                        for ky in range(3)
                    ],
                    axis=1,
                )
                for z in range(2)
            ],
            axis=0,
        )
        res = jnp.dot(lhs, w3[...], preferred_element_type=F32)
        top = jnp.maximum(res[:, :128], res[:, 128:]).reshape(2, nt, 2, 64, 128)
        top = jnp.maximum(top[:, :, 0], top[:, :, 1])
        top = jnp.maximum(top + b3, 0.0)
        for z in range(2):
            for r in range(nt):
                third[z, r] = top[z, r]
            for r in range(nt, TILE[c]):
                third[z, r] = jnp.zeros((64, 128), F32)
        outside(third, c, (0, 1), (nt - 1, nt))
        for z in range(2):
            for x0 in range(0, 64, 8):
                block = third[z, : TILE[c], x0 : x0 + 8, :]
                slab[c][1 + x0 : 9 + x0, z] = jnp.transpose(block, (1, 0, 2)).astype(BF16)

        own_copy(c).start()

        @pl.loop(1, nx)
        def _(k):
            turn_copy(c, k).start()

    def side_copy(dx, g):
        k = (dx + 1) // 2
        rows = pl.ds(1 + 4 * g, 4)
        return pltpu.make_async_remote_copy(
            src_ref=mid.at[1, 1 if dx == -1 else 2, rows],
            dst_ref=mid.at[1, 3 if dx == -1 else 0, rows],
            send_sem=side_send.at[k, g], recv_sem=side_recv.at[k, g],
            device_id=(me + dx, yi), device_id_type=MESH,
        )

    def edge_copy(dy):
        k = (dy + 1) // 2
        return pltpu.make_async_remote_copy(
            src_ref=mid.at[1, pl.ds(1, 2), 1 if dy == -1 else 16],
            dst_ref=mid.at[1, pl.ds(1, 2), 17 if dy == -1 else 0],
            send_sem=edge_send.at[k], recv_sem=edge_recv.at[k],
            device_id=(me, yi + dy), device_id_type=MESH,
        )

    def corner_copy(dx, dy):
        k, j = (dx + 1) // 2, (dy + 1) // 2
        return pltpu.make_async_remote_copy(
            src_ref=mid.at[1, 1 if dx == -1 else 2, 1 if dy == -1 else 16],
            dst_ref=mid.at[1, 3 if dx == -1 else 0, 17 if dy == -1 else 0],
            send_sem=corner_send.at[k, j], recv_sem=corner_recv.at[k, j],
            device_id=(me + dx, yi + dy), device_id_type=MESH,
        )

    def send_sides(g):
        for dx in (-1, 1):

            @pl.when(hasx[dx])
            def _():
                side_copy(dx, g).start()

    def send_edges(dy):
        @pl.when(has[dy])
        def _():
            edge_copy(dy).start()

        for dx in (-1, 1):

            @pl.when(jnp.logical_and(has[dy], hasx[dx]))
            def _():
                corner_copy(dx, dy).start()

    def cube_rows(source, weight, y, rows, chans):
        lhs = jnp.concatenate(
            [
                jnp.concatenate(
                    [
                        source[kz, x + kx, y + ky : y + ky + rows].reshape(64 * rows, chans)
                        for kz in range(3)
                        for ky in range(3)
                        for kx in range(3)
                    ],
                    axis=1,
                )
                for x in range(2)
            ],
            axis=0,
        )
        return jnp.dot(lhs, weight[...], preferred_element_type=F32)

    ba, bb = small[12:13, :], small[13:14, :]
    load_a.wait()
    for c, (y_begin, y_end) in enumerate(((0, 4), (4, 12), (12, 16))):
        t_begin, t_end = CHUNKS[c][2]
        own_copy(c).wait()

        @pl.loop(1, nx)
        def _(k):
            turn_copy(c, k).wait_recv()

        for x in range(4):
            rows = jnp.transpose(brick[c][x].astype(F32), (1, 0, 2))
            for r in range(t_end - t_begin):
                down, up = shifted(rows[r])
                tall[0, x, t_begin + r] = down.astype(BF16)
                tall[1, x, t_begin + r] = rows[r].astype(BF16)
                tall[2, x, t_begin + r] = up.astype(BF16)

        for y in range(y_begin, y_end, 4):
            res = cube_rows(tall, wa, y, 4, 128)
            res = jnp.maximum(res + ba, 0.0).reshape(2, 4, 64, 256)
            for x in range(2):
                for r in range(4):
                    down, up = shifted(res[x, r])
                    mid[0, 1 + x, 1 + y + r] = down.astype(BF16)
                    mid[1, 1 + x, 1 + y + r] = res[x, r].astype(BF16)
                    mid[2, 1 + x, 1 + y + r] = up.astype(BF16)
            send_sides(y // 4)

        if c == 0:
            send_edges(-1)
        if c == 2:
            send_edges(1)

    def spread_row(x, r):
        down, up = shifted(mid[1, x, r].astype(F32))
        mid[0, x, r] = down.astype(BF16)
        mid[2, x, r] = up.astype(BF16)

    def take_sides(g):
        for dx in (-1, 1):

            @pl.when(hasx[-dx])
            def _():
                side_copy(dx, g).wait_recv()
                for r in range(4):
                    spread_row(3 if dx == -1 else 0, 1 + 4 * g + r)

    def take_edges(dy):
        row = 17 if dy == -1 else 0

        @pl.when(has[-dy])
        def _():
            edge_copy(dy).wait_recv()
            spread_row(1, row)
            spread_row(2, row)

        for dx in (-1, 1):

            @pl.when(jnp.logical_and(has[-dy], hasx[-dx]))
            def _():
                corner_copy(dx, dy).wait_recv()
                spread_row(3 if dx == -1 else 0, row)

    def last_rows(y):
        res = cube_rows(mid, wb, y, 4, 256)
        res = jnp.maximum(res + bb, 0.0).astype(BF16).reshape(2, 4, 64, 256)
        for x in range(2):
            for r in range(4):
                out[x, y + r] = res[x, r]

    load_b.wait()
    take_sides(0)
    take_sides(1)
    take_sides(2)
    last_rows(4)
    take_sides(3)
    last_rows(8)
    take_edges(-1)
    last_rows(12)
    take_edges(1)
    last_rows(0)

    for c in range(3):

        @pl.loop(1, nx)
        def _(k):
            turn_copy(c, k).wait_send()

    for dx in (-1, 1):

        @pl.when(hasx[dx])
        def _():
            @pl.loop(0, 4)
            def _(g):
                side_copy(dx, g).wait_send()

    for dy in (-1, 1):

        @pl.when(has[dy])
        def _():
            edge_copy(dy).wait_send()

        for dx in (-1, 1):

            @pl.when(jnp.logical_and(has[dy], hasx[dx]))
            def _():
                corner_copy(dx, dy).wait_send()


def body(raw, wf, bf, ws, bs, wt, bt, wa, ba, wb, bb):
    nx, ny = lax.axis_size("gz"), lax.axis_size("xy")
    dma = pltpu.SemaphoreType.DMA
    taps = jnp.transpose(wf.reshape(32, 9)).astype(F32)
    small = jnp.concatenate(
        [
            jnp.tile(taps, (1, 8)),
            jnp.tile(bf, 8)[None],
            jnp.tile(bs, 4)[None],
            jnp.tile(bt, 2)[None],
            ba[None],
            bb[None],
            jnp.zeros((2, 256), F32),
        ],
        axis=0,
    )
    out = pl.pallas_call(
        functools.partial(kernel, nx, ny),
        name="encoder",
        out_shape=jax.ShapeDtypeStruct((2, 16, 64, 256), BF16),
        in_specs=[VMEM] * 4 + [ANY, ANY],
        out_specs=VMEM,
        scratch_shapes=[
            pltpu.VMEM((2, ROWS, 512), BF16),
            pltpu.VMEM((512, 768), BF16),
            pltpu.VMEM((16, 256, 256), BF16),
            pltpu.VMEM((2, ROWS, 768), F32),
            pltpu.VMEM((WINS, 2, 128, 256), BF16),
            pltpu.VMEM((2, 80, 128, 128), BF16),
            pltpu.VMEM((2, 38, 64, 256), BF16),
            pltpu.VMEM((2, 8, 64, 128), F32),
        ]
        + [pltpu.VMEM((66, 2, rows, 128), BF16) for rows in TILE]
        + [pltpu.VMEM((4, 64, rows, 128), BF16) for rows in TILE]
        + [
            pltpu.VMEM((3, 4, 18, 64, 128), BF16),
            pltpu.VMEM((3, 4, 18, 64, 256), BF16),
            pltpu.VMEM((27 * 128, 256), BF16),
            pltpu.VMEM((27 * 256, 256), BF16),
            dma((2,)), dma((2,)), dma((3, nx)), dma((3, nx)), dma((3,)), dma((2,)),
            dma((2, 4)), dma((2, 4)), dma((2,)), dma((2,)), dma((2, 2)), dma((2, 2)),
        ],
        compiler_params=pltpu.CompilerParams(
            collective_id=0, has_side_effects=True, vmem_limit_bytes=60 << 20
        ),
    )(
        raw,
        small,
        banded_second(ws),
        banded_third(wt),
        wa.reshape(27 * 128, 256),
        wb.reshape(27 * 256, 256),
    )
    return jnp.transpose(out, (2, 1, 0, 3))


def solution(mesh):
    placed = (P("gz", "xy", None), P(), P(), P(), P(), P(), P(), P(), P(), P(), P())
    return jax.shard_map(
        body, mesh=mesh, in_specs=placed, out_specs=P(None, "xy", "gz", None), check_vma=False
    )
```

time: 85.3 us -> 84 us (0.985)
  the two profiles are of different devices: /device:TPU:25 before, /device:TPU:16 now
where the time goes in v2:
time: 84 us; the launch traced here: 82.9 us
  Pallas kernels  70.9 us (84%)
  local copies, waits for them, and re-layouts  10.3 us (12%)
  other arithmetic  1.69 us (2%)
    pallas_call x1, Pallas kernels, body(): pl.pallas_call(functools.partial(kernel, nx, ny), name='encoder', out_sha...  70.9 us
    transpose x1, local copies, waits for them, and re-layouts, body(): return jnp.transpose(out, (2, 1, 0, 3))  3.28 us
    concatenate x1, local copies, waits for them, and re-layouts, body(): jnp.concatenate([jnp.tile(taps, (1, 8)), jnp.tile(bf, 8)[None], jnp.tile(...  1.93 us

profile of v2, /device:TPU:16, one launch (start us, length us, event | category | flops | bytes accessed | tf_op | source)
XLA Modules:
  0.0 82.9 jit_solution(12693839935268483364)
XLA Ops:
  0.0 0.7 tile.14
  0.7 0.7 tile.13
  1.3 0.1 broadcast_in_dim_tile.10
  1.4 0.7 tile.12
  2.1 0.1 broadcast_in_dim_tile.9
  2.1 0.7 reshape.42
  2.8 0.1 tile.11
  2.9 1.9 %concatenate.9.small = f32[16,256]{1,0:T(8,128)} concatenate(f32[9,256]{1,0:T(8,128)S(1)} %tile.11, f32[1,256]{1,0:T(1,128)S(1)} %broadcast_in_dim_tile.9, f32[1,256]{1,0:T(1,128)S(1)} %broadcast_in_dim_tile.10, f32[1,256]{1,0:T(1,128)S(1)} %bitcast.31, f32[1,256]{1,0:T(1,128)} %bitcast.29, f32[1,256]{1,0:T(1,128)} %bitcast.30, f32[2,256]{1,0:T(2,128)S(1)} %broadcast_in_dim.11), dimensions={0} | concatenate | bytes 32768 | tf_op jit(solution)/shard_map/concatenate | solution.py:473
  4.8 1.0 %fusion = (bf16[3,4,64,128]{3,2,1,0:T(8,128)(2,1)S(1)}, bf16[3,4,64,128]{3,2,1,0:T(8,128)(2,1)S(1)}) fusion(bf16[3,3,64,128]{3,2,1,0:T(8,128)(2,1)} %bitcast.26), kind=kLoop, calls=%fused_computation.2 | loop fusion | bytes 540672 | tf_op jit(solution)/shard_map/jit(_pad)/pad | solution.py:33
  5.9 0.8 pad_maximum_fusion.w3
  6.7 1.1 %fusion.1 = (bf16[4,4,32,64]{3,2,1,0:T(8,128)(2,1)S(1)}, bf16[4,4,32,64]{3,2,1,0:T(8,128)(2,1)S(1)}, bf16[4,4,32,64]{3,2,1,0:T(8,128)(2,1)S(1)}, bf16[4,4,32,64]{3,2,1,0:T(8,128)(2,1)S(1)}) fusion(bf16[3,3,32,64]{3,2,1,0:T(8,128)(2,1)} %bitcast.27), kind=kLoop, calls=%fused_computation.3 | loop fusion | bytes 299008 | tf_op jit(solution)/shard_map/jit(_pad)/pad | solution.py:24
  7.8 0.9 %pad_maximum_fusion.1.w2 = bf16[512,256]{1,0:T(8,128)(2,1)} fusion(bf16[512,64]{1,0:T(8,128)(2,1)S(1)} %bitcast.23, bf16[512,64]{1,0:T(8,128)(2,1)S(1)} %bitcast.24, bf16[512,64]{1,0:T(8,128)(2,1)S(1)} %bitcast.25, bf16[512,64]{1,0:T(8,128)(2,1)S(1)} %bitcast.22), kind=kLoop, calls=%fused_computation.1 | loop fusion | flops 1048576 | bytes 524288 | tf_op jit(solution)/shard_map/concatenate | solution.py:28
  8.7 70.9 %encoder.1 = bf16[2,16,64,256]{3,2,1,0:T(8,128)(2,1)} custom-call(bf16[2,128,512]{2,1,0:T(8,128)(2,1)} %raw.1, f32[16,256]{1,0:T(8,128)} %concatenate.9.small, bf16[512,256]{1,0:T(8,128)(2,1)} %pad_maximum_fusion.1.w2, bf16[768,256]{1,0:T(8,128)(2,1)} %pad_maximum_fusion.w3, bf16[3456,256]{1,0:T(8,128)(2,1)} %bitcast.19, bf16[6912,256]{1,0:T(8,128)(2,1)} %bitcast.18), custom_call_target="tpu_custom_call" | custom-call | tf_op jit(solution)/shard_map/encoder/pallas_call | solution.py:485
  79.6 3.3 %copy.12 = bf16[64,16,2,256]{3,2,1,0:T(2,128)(2,1)} copy(bf16[64,16,2,256]{3,0,1,2:T(8,128)(2,1)} %bitcast.17) | data formatting | bytes 2097152 | tf_op jit(solution)/shard_map/transpose | solution.py:522
  (2 shorter events, 0.0 us)

commit v3 on v2

v3 whole, which is shorter than its diff:
```python
import functools

import jax
import jax.numpy as jnp
from jax import lax
from jax.experimental import pallas as pl
from jax.experimental.pallas import tpu as pltpu
from jax.sharding import PartitionSpec as P

F32 = jnp.float32
BF16 = jnp.bfloat16
MESH = pl.DeviceIdType.MESH
VMEM = pl.BlockSpec(memory_space=pltpu.VMEM)
ANY = pl.BlockSpec(memory_space=pl.ANY)
ROWS = 168
WINS = (1, 2, 3, 0, 4)
CHUNKS = (((12, 30), (6, 14), 8), ((0, 12), (0, 6), 8), ((30, 38), (14, 18), 4))
GROUPS = ((0, 6, 3), (0, 9, 3), (1, 3, 3), (1, 0, 3), (2, 12, 4))


def shifted(rows):
    sub = lax.broadcasted_iota(jnp.int32, rows.shape, 0)
    last = rows.shape[0] - 1
    down = jnp.where(sub == 0, 0.0, pltpu.roll(rows, 1, 0))
    up = jnp.where(sub == last, 0.0, pltpu.roll(rows, last, 0))
    return down, up


def make_pick(pick):
    source = lax.broadcasted_iota(jnp.int32, (512, 128), 0)
    m = lax.broadcasted_iota(jnp.int32, (512, 128), 1)
    start = 8 * jnp.where(m < 64, m, m - 64) + jnp.where(m < 64, 0, 4) - 1
    gap = source - start
    for j in range(6):
        pick[:, 128 * j : 128 * j + 128] = jnp.where(gap == j, 1.0, 0.0).astype(BF16)


def make_small(wf, small):
    for ky in range(3):
        for kx in range(3):
            row = wf[ky, kx : kx + 1, :].astype(F32)
            small[3 * ky + kx : 3 * ky + kx + 1, :] = jnp.concatenate([row] * 8, axis=1)


def make_first(small, w1):
    lane = lax.broadcasted_iota(jnp.int32, (1, 256), 1)
    bit = lambda n: jnp.where(jnp.bitwise_and(lane, n) == 0, 0, 1)
    start = 2 * (1 - bit(32)) + bit(64)
    cols = []
    for j in range(6):
        for ky in range(3):
            total = jnp.zeros((1, 256), F32)
            for kx in range(3):
                total = jnp.where(start == j - kx, small[3 * ky + kx : 3 * ky + kx + 1, :], total)
            cols.append(jnp.broadcast_to(total, (40, 256)))
    wide = lax.broadcasted_iota(jnp.int32, (40, 256), 1)
    gap = lax.broadcasted_iota(jnp.int32, (40, 256), 0) - jnp.where(wide < 128, 1, 2)

    @pl.loop(0, 16)
    def _(i):
        hit = [gap == 2 * i + ky for ky in range(3)]
        for j in range(6):
            total = jnp.zeros((40, 256), F32)
            for ky in range(3):
                total = jnp.where(hit[ky], cols[3 * j + ky], total)
            w1[i, 40 * j : 40 * j + 40] = total.astype(BF16)
        w1[i, 240:] = jnp.zeros((16, 256), BF16)


def make_second(ws, w2):
    w2[...] = jnp.zeros((512, 256), BF16)
    for py in range(2):
        for px in range(2):
            lanes = slice(64 * (2 * py + px), 64 * (2 * py + px) + 64)
            for ky in range(3):
                for kx in range(3):
                    row = 32 * (4 * (ky + py) + kx + px)
                    w2[row : row + 32, lanes] = ws[ky, kx]


def make_third(wt, w3):
    w3[...] = jnp.zeros((768, 256), BF16)
    for px in range(2):
        for ky in range(3):
            for kx in range(3):
                row = 256 * ky + 64 * (kx + px)
                w3[row : row + 64, 128 * px : 128 * px + 128] = wt[ky, kx]


def kernel(
    nx, ny, raw, wf, bf, ws, bs, wt, bt, wa_hbm, ba, wb_hbm, bb,
    out,
    above, below, small, pick, w1, w2, w3, spread, turned, first, second, third,
    slab_0, slab_1, slab_2, brick_0, brick_1, brick_2, tall, mid, wa, wb,
    raw_send, raw_recv, turn_send, turn_recv, own_sem, load_sem,
    side_send, side_recv, edge_send, edge_recv, corner_send, corner_recv,
):
    me = lax.axis_index("gz")
    yi = lax.axis_index("xy")
    slab, brick = (slab_0, slab_1, slab_2), (brick_0, brick_1, brick_2)
    has = {-1: yi > 0, 1: yi < ny - 1}
    hasx = {-1: me > 0, 1: me < nx - 1}

    load_a = pltpu.make_async_copy(wa_hbm, wa, load_sem.at[0])
    load_b = pltpu.make_async_copy(wb_hbm, wb, load_sem.at[1])
    load_a.start()
    load_b.start()

    barrier = pltpu.get_barrier_semaphore()

    def greet(gx, gy):
        pl.semaphore_signal(barrier, inc=1, device_id=(gx, gy), device_id_type=MESH)

    @pl.loop(1, nx)
    def _(k):
        greet(lax.rem(me + k, nx), yi)

    for dy in (-1, 1):

        @pl.when(has[dy])
        def _():
            greet(me, yi + dy)

        for dx in (-1, 1):

            @pl.when(jnp.logical_and(has[dy], hasx[dx]))
            def _():
                greet(me + dx, yi + dy)

    make_small(wf, small)
    make_pick(pick)
    make_first(small, w1)
    make_second(ws, w2)
    make_third(wt, w3)
    for z in range(2):
        spread[z, 16:144] = jnp.dot(raw[z], pick[...], preferred_element_type=F32)

    one = lambda flag: jnp.where(flag, 1, 0)
    tall_n = one(has[-1]) + one(has[1])
    wide_n = one(hasx[-1]) + one(hasx[1])
    pl.semaphore_wait(barrier, nx - 1 + tall_n + tall_n * wide_n)

    def raw_copy(dy):
        k = (dy + 1) // 2
        return pltpu.make_async_remote_copy(
            src_ref=raw.at[:, pl.ds(112 if dy == 1 else 0, 16)],
            dst_ref=above if dy == 1 else below,
            send_sem=raw_send.at[k], recv_sem=raw_recv.at[k],
            device_id=(me, yi + dy), device_id_type=MESH,
        )

    for dy in (-1, 1):

        @pl.when(has[dy])
        def _():
            raw_copy(dy).start()

        @pl.when(jnp.logical_not(has[dy]))
        def _():
            (above if dy == -1 else below)[...] = jnp.zeros((2, 16, 512), BF16)

    for dx in (-1, 1):

        @pl.when(jnp.logical_not(hasx[dx]))
        def _():
            col = 0 if dx == -1 else 3

            @pl.loop(0, 18)
            def _(r):
                for kz in range(3):
                    mid[kz, col, r] = jnp.zeros((64, 256), BF16)

    for dy in (-1, 1):

        @pl.when(jnp.logical_not(has[dy]))
        def _():
            row = 0 if dy == -1 else 17
            for kz in range(3):
                for x in range(4):
                    mid[kz, x, row] = jnp.zeros((64, 256), BF16)

    for c in range(3):
        slab[c][0] = jnp.zeros((2, CHUNKS[c][2], 128), BF16)
        slab[c][65] = jnp.zeros((2, CHUNKS[c][2], 128), BF16)

    lane64 = lax.broadcasted_iota(jnp.int32, (64, 128), 1)
    low, high, half = lane64 < 32, lane64 >= 96, lane64 < 64
    b1 = jnp.concatenate([bf[...]] * 4, axis=1)
    b2 = jnp.concatenate([bs[...]] * 2, axis=1)
    b3 = bt[...]

    def sent(c):
        (t_begin, t_end), stored = CHUNKS[c][1:]
        return pl.ds(0, t_end - t_begin)

    def turn_copy(c, k):
        there = lax.rem(me + k, nx)
        return pltpu.make_async_remote_copy(
            src_ref=slab[c].at[pl.ds(2 * there, 4), :, sent(c)],
            dst_ref=brick[c].at[:, pl.ds(2 * me, 2), sent(c)],
            send_sem=turn_send.at[c, k],
            recv_sem=turn_recv.at[c, k],
            device_id=(there, yi),
            device_id_type=MESH,
        )

    def own_copy(c):
        return pltpu.make_async_copy(
            slab[c].at[pl.ds(2 * me, 4), :, sent(c)],
            brick[c].at[:, pl.ds(2 * me, 2), sent(c)],
            own_sem.at[c],
        )

    def blank(ref, begin, end):
        for z in range(2):
            for r in range(begin, end):
                ref[z, r] = jnp.zeros(ref.shape[2:], ref.dtype)

    def blank_low(ref, begin, end):
        pl.when(jnp.logical_not(has[-1]))(lambda: blank(ref, begin, end))

    def blank_high(ref, begin, end):
        pl.when(jnp.logical_not(has[1]))(lambda: blank(ref, begin, end))

    def first_level(begin, end):
        wins = end - begin
        for n in range(begin, end):
            for z in range(2):
                rows = slice(WINS[n] * 32, WINS[n] * 32 + 40)
                parts = [spread[z, rows, j * 128 : (j + 1) * 128] for j in range(6)]
                parts.append(jnp.zeros((16, 128), F32))
                turned[n, z] = jnp.concatenate(parts, axis=0).T.astype(BF16)
        for i in range(16):
            lhs = turned[begin:end].reshape(wins * 256, 256)
            res = jnp.dot(lhs, w1[i], preferred_element_type=F32)
            top = jnp.maximum(res[:, :128], res[:, 128:])
            top = jnp.maximum(top, pltpu.roll(top, 64, 1))
            top = jnp.maximum(top + b1, 0.0).reshape(wins, 2, 128, 128)
            for w in range(wins):
                for z in range(2):
                    even, odd = top[w, z, :64], top[w, z, 64:]
                    down, up = shifted(odd)[0], shifted(even)[1]
                    row = 16 * WINS[begin + w] + i
                    left = jnp.where(low, down, jnp.where(high, odd, even))
                    right = jnp.where(low, even, jnp.where(high, up, odd))
                    first[z, row, :64] = left.astype(BF16)
                    first[z, row, 64:] = right.astype(BF16)

    def second_level(begin, end):
        for q0 in range(begin, end, 2):
            lhs = jnp.concatenate(
                [
                    jnp.concatenate([first[z, 2 * (q0 + k) + a] for a in range(4)], axis=1)
                    for z in range(2)
                    for k in range(2)
                ],
                axis=0,
            )
            res = jnp.dot(lhs, w2[...], preferred_element_type=F32)
            top = jnp.maximum(res[:, :128], res[:, 128:])
            top = jnp.maximum(top, pltpu.roll(top, 64, 1))
            top = jnp.maximum(top + b2, 0.0).reshape(2, 2, 128, 128)
            for k in range(2):
                for z in range(2):
                    even, odd = top[z, k, :64], top[z, k, 64:]
                    down, up = shifted(odd)[0], shifted(even)[1]
                    second[z, q0 + k, :, :128] = jnp.where(half, down, even).astype(BF16)
                    second[z, q0 + k, :, 128:] = jnp.where(half, odd, up).astype(BF16)

    def third_level(begin, end):
        nt = end - begin
        lhs = jnp.concatenate(
            [
                jnp.concatenate(
                    [
                        second[z, 2 * begin + ky : 2 * end + ky].reshape(nt * 128, 256)
                        for ky in range(3)
                    ],
                    axis=1,
                )
                for z in range(2)
            ],
            axis=0,
        )
        res = jnp.dot(lhs, w3[...], preferred_element_type=F32)
        top = jnp.maximum(res[:, :128], res[:, 128:]).reshape(2, nt, 2, 64, 128)
        top = jnp.maximum(top[:, :, 0], top[:, :, 1])
        top = jnp.maximum(top + b3, 0.0)
        for z in range(2):
            for r in range(nt):
                third[z, r] = top[z, r]

    def send(c):
        for z in range(2):
            for x0 in range(0, 64, 8):
                block = third[z, : CHUNKS[c][2], x0 : x0 + 8, :]
                slab[c][1 + x0 : 9 + x0, z] = jnp.transpose(block, (1, 0, 2)).astype(BF16)
        own_copy(c).start()

        @pl.loop(1, nx)
        def _(k):
            turn_copy(c, k).start()

    first_level(0, 3)
    second_level(*CHUNKS[0][0])
    third_level(*CHUNKS[0][1])
    send(0)

    for dy in (-1, 1):

        @pl.when(has[dy])
        def _():
            raw_copy(dy).wait_send()

        @pl.when(has[-dy])
        def _():
            raw_copy(dy).wait_recv()

    for z in range(2):
        rows = jnp.concatenate([above[z], below[z], jnp.zeros((16, 512), BF16)], axis=0)
        res = jnp.dot(rows, pick[...], preferred_element_type=F32)
        spread[z, :16] = res[:16]
        spread[z, 144:168] = res[16:40]
    first_level(3, 5)
    blank_low(first, 0, 7)
    blank_high(first, 71, 80)
    second_level(*CHUNKS[1][0])
    blank_low(second, 0, 3)
    third_level(*CHUNKS[1][1])
    blank_low(third, 0, 1)
    send(1)
    second_level(*CHUNKS[2][0])
    blank_high(second, 35, 38)
    third_level(*CHUNKS[2][1])
    blank_high(third, 3, 4)
    send(2)

    def side_copy(dx, g):
        k = (dx + 1) // 2
        rows = pl.ds(1 + GROUPS[g][1], GROUPS[g][2])
        return pltpu.make_async_remote_copy(
            src_ref=mid.at[1, 1 if dx == -1 else 2, rows],
            dst_ref=mid.at[1, 3 if dx == -1 else 0, rows],
            send_sem=side_send.at[k, g], recv_sem=side_recv.at[k, g],
            device_id=(me + dx, yi), device_id_type=MESH,
        )

    def edge_copy(dy):
        k = (dy + 1) // 2
        return pltpu.make_async_remote_copy(
            src_ref=mid.at[1, pl.ds(1, 2), 1 if dy == -1 else 16],
            dst_ref=mid.at[1, pl.ds(1, 2), 17 if dy == -1 else 0],
            send_sem=edge_send.at[k], recv_sem=edge_recv.at[k],
            device_id=(me, yi + dy), device_id_type=MESH,
        )

    def corner_copy(dx, dy):
        k, j = (dx + 1) // 2, (dy + 1) // 2
        return pltpu.make_async_remote_copy(
            src_ref=mid.at[1, 1 if dx == -1 else 2, 1 if dy == -1 else 16],
            dst_ref=mid.at[1, 3 if dx == -1 else 0, 17 if dy == -1 else 0],
            send_sem=corner_send.at[k, j], recv_sem=corner_recv.at[k, j],
            device_id=(me + dx, yi + dy), device_id_type=MESH,
        )

    def send_sides(g):
        for dx in (-1, 1):

            @pl.when(hasx[dx])
            def _():
                side_copy(dx, g).start()

    def send_edges(dy):
        @pl.when(has[dy])
        def _():
            edge_copy(dy).start()

        for dx in (-1, 1):

            @pl.when(jnp.logical_and(has[dy], hasx[dx]))
            def _():
                corner_copy(dx, dy).start()

    def cube_rows(source, weight, runs, chans):
        lhs = jnp.concatenate(
            [
                jnp.concatenate(
                    [
                        source[kz, x + kx, y + ky : y + ky + rows].reshape(64 * rows, chans)
                        for kz in range(3)
                        for ky in range(3)
                        for kx in range(3)
                    ],
                    axis=1,
                )
                for x in range(2)
                for y, rows in runs
            ],
            axis=0,
        )
        return jnp.dot(lhs, weight[...], preferred_element_type=F32)

    load_a.wait()
    arrived = -1
    for g, (c, y, rows) in enumerate(GROUPS):
        if c != arrived:
            arrived = c
            own_copy(c).wait()

            @pl.loop(1, nx)
            def _(k):
                turn_copy(c, k).wait_recv()

            t_begin, t_end = CHUNKS[c][1]
            for x in range(4):
                lines = jnp.transpose(brick[c][x].astype(F32), (1, 0, 2))
                for r in range(t_end - t_begin):
                    down, up = shifted(lines[r])
                    tall[0, x, t_begin + r] = down.astype(BF16)
                    tall[1, x, t_begin + r] = lines[r].astype(BF16)
                    tall[2, x, t_begin + r] = up.astype(BF16)

        res = cube_rows(tall, wa, ((y, rows),), 128)
        res = jnp.maximum(res + ba[...], 0.0).reshape(2, rows, 64, 256)
        for x in range(2):
            for r in range(rows):
                down, up = shifted(res[x, r])
                mid[0, 1 + x, 1 + y + r] = down.astype(BF16)
                mid[1, 1 + x, 1 + y + r] = res[x, r].astype(BF16)
                mid[2, 1 + x, 1 + y + r] = up.astype(BF16)
        if y == 0:
            send_edges(-1)
        if y == 12:
            send_edges(1)
        send_sides(g)

    def spread_row(x, r):
        down, up = shifted(mid[1, x, r].astype(F32))
        mid[0, x, r] = down.astype(BF16)
        mid[2, x, r] = up.astype(BF16)

    def take_sides(g):
        for dx in (-1, 1):

            @pl.when(hasx[-dx])
            def _():
                side_copy(dx, g).wait_recv()
                for r in range(GROUPS[g][2]):
                    spread_row(3 if dx == -1 else 0, 1 + GROUPS[g][1] + r)

    def take_edges(dy):
        row = 17 if dy == -1 else 0

        @pl.when(has[-dy])
        def _():
            edge_copy(dy).wait_recv()
            spread_row(1, row)
            spread_row(2, row)

        for dx in (-1, 1):

            @pl.when(jnp.logical_and(has[-dy], hasx[-dx]))
            def _():
                corner_copy(dx, dy).wait_recv()
                spread_row(3 if dx == -1 else 0, row)

    def last_rows(*runs):
        res = cube_rows(mid, wb, runs, 256)
        res = jnp.maximum(res + bb[...], 0.0).reshape(2, -1, 64, 256)
        lines = [y + r for y, rows in runs for r in range(rows)]
        for x in range(2):
            for r, line in enumerate(lines):
                out[:, line, x] = res[x, r].astype(BF16)

    load_b.wait()
    take_sides(0)
    take_sides(1)
    last_rows((7, 4))
    take_sides(2)
    last_rows((4, 3))
    take_sides(3)
    last_rows((1, 3))
    take_sides(4)
    last_rows((11, 4))
    take_edges(-1)
    take_edges(1)
    last_rows((0, 1), (15, 1))

    for c in range(3):

        @pl.loop(1, nx)
        def _(k):
            turn_copy(c, k).wait_send()

    for dx in (-1, 1):

        @pl.when(hasx[dx])
        def _():
            for g in range(5):
                side_copy(dx, g).wait_send()

    for dy in (-1, 1):

        @pl.when(has[dy])
        def _():
            edge_copy(dy).wait_send()

        for dx in (-1, 1):

            @pl.when(jnp.logical_and(has[dy], hasx[dx]))
            def _():
                corner_copy(dx, dy).wait_send()


def body(raw, wf, bf, ws, bs, wt, bt, wa, ba, wb, bb):
    nx, ny = lax.axis_size("gz"), lax.axis_size("xy")
    dma = pltpu.SemaphoreType.DMA
    return pl.pallas_call(
        functools.partial(kernel, nx, ny),
        name="encoder",
        out_shape=jax.ShapeDtypeStruct((64, 16, 2, 256), BF16),
        in_specs=[VMEM] * 7 + [ANY, VMEM, ANY, VMEM],
        out_specs=VMEM,
        scratch_shapes=[
            pltpu.VMEM((2, 16, 512), BF16),
            pltpu.VMEM((2, 16, 512), BF16),
            pltpu.VMEM((16, 256), F32),
            pltpu.VMEM((512, 768), BF16),
            pltpu.VMEM((16, 256, 256), BF16),
            pltpu.VMEM((512, 256), BF16),
            pltpu.VMEM((768, 256), BF16),
            pltpu.VMEM((2, ROWS, 768), F32),
            pltpu.VMEM((len(WINS), 2, 128, 256), BF16),
            pltpu.VMEM((2, 80, 128, 128), BF16),
            pltpu.VMEM((2, 38, 64, 256), BF16),
            pltpu.VMEM((2, 8, 64, 128), F32),
        ]
        + [pltpu.VMEM((66, 2, stored, 128), BF16) for _, _, stored in CHUNKS]
        + [pltpu.VMEM((4, 64, stored, 128), BF16) for _, _, stored in CHUNKS]
        + [
            pltpu.VMEM((3, 4, 18, 64, 128), BF16),
            pltpu.VMEM((3, 4, 18, 64, 256), BF16),
            pltpu.VMEM((27 * 128, 256), BF16),
            pltpu.VMEM((27 * 256, 256), BF16),
            dma((2,)), dma((2,)), dma((3, nx)), dma((3, nx)), dma((3,)), dma((2,)),
            dma((2, 5)), dma((2, 5)), dma((2,)), dma((2,)), dma((2, 2)), dma((2, 2)),
        ],
        compiler_params=pltpu.CompilerParams(
            collective_id=0, has_side_effects=True, vmem_limit_bytes=60 << 20
        ),
    )(
        raw,
        jnp.transpose(wf[:, 0], (1, 2, 0)),
        bf.reshape(1, 32),
        jnp.transpose(ws, (2, 3, 1, 0)),
        bs.reshape(1, 64),
        jnp.transpose(wt, (2, 3, 1, 0)),
        bt.reshape(1, 128),
        wa.reshape(27 * 128, 256),
        ba.reshape(1, 256),
        wb.reshape(27 * 256, 256),
        bb.reshape(1, 256),
    )


def solution(mesh):
    placed = (P("gz", "xy", None), P(), P(), P(), P(), P(), P(), P(), P(), P(), P())
    return jax.shard_map(
        body, mesh=mesh, in_specs=placed, out_specs=P(None, "xy", "gz", None), check_vma=False
    )
```

time: 84 us -> 71.3 us (0.85); the launches traced: 82.9 us -> 71.2 us
  local copies, waits for them, and re-layouts: 10.3 us -> 3.13 us
  Pallas kernels: 70.9 us -> 68.1 us
  other arithmetic: 1.69 us -> 0 us
    transpose x1 -> x0, local copies, waits for them, and re-layouts: 3.28 us -> none  [body(): return jnp.transpose(out, (2, 1, 0, 3))]
    unnamed x0 -> x1, local copies, waits for them, and re-layouts: none -> 3.13 us
    pallas_call x1, Pallas kernels: 70.9 us -> 68.1 us  [body(): pl.pallas_call(functools.partial(kernel, nx, ny), name='encoder', out_sha...]
    another operation x7 -> x0, local copies, waits for them, and re-layouts: 2.22 us -> none  [the longest x2 0.74 us: body(): jnp.tile(bs, 4)[None]]
    pad x2 -> x0, local copies, waits for them, and re-layouts: 2.14 us -> none  [the longest x1 1.12 us: banded_second(): jnp.pad(taps, ((py, 1 - py), (px, 1 - px), (0, 0), (0, 0))).reshape(512, 64)]
    concatenate x1 -> x0, local copies, waits for them, and re-layouts: 1.93 us -> none  [body(): jnp.concatenate([jnp.tile(taps, (1, 8)), jnp.tile(bf, 8)[None], jnp.tile(...]
    concatenate x2 -> x0, other arithmetic: 1.69 us -> none  [the longest x1 0.9 us: banded_second(): return jnp.concatenate(parts, axis=1)]
where the time goes in v3:
time: 71.3 us; the launch traced here: 71.2 us
  Pallas kernels  68.1 us (96%)
  local copies, waits for them, and re-layouts  3.13 us (4%)
    pallas_call x1, Pallas kernels, body(): pl.pallas_call(functools.partial(kernel, nx, ny), name='encoder', out_sha...  68.1 us
    unnamed x1, local copies, waits for them, and re-layouts  3.13 us

profile of v3, /device:TPU:16, one launch (start us, length us, event | category | flops | bytes accessed | tf_op | source)
XLA Modules:
  0.0 71.2 jit_solution(2360077306846580205)
XLA Ops:
  0.0 68.1 %encoder.1 = bf16[64,16,2,256]{3,2,1,0:T(2,128)(2,1)} custom-call(bf16[2,128,512]{2,1,0:T(8,128)(2,1)} %raw.1, bf16[3,3,32]{2,1,0:T(4,128)(2,1)} %bitcast.16, f32[1,32]{1,0:T(1,128)} %bitcast.19, bf16[3,3,32,64]{3,2,1,0:T(8,128)(2,1)} %bitcast.15, f32[1,64]{1,0:T(1,128)} %bitcast.20, bf16[3,3,64,128]{3,2,1,0:T(8,128)(2,1)} %bitcast.14, f32[1,128]{1,0:T(1,128)} %bitcast.21, ...), custom_call_target="tpu_custom_call" | custom-call | tf_op jit(solution)/shard_map/encoder/pallas_call | solution.py:518
  68.1 3.1 %copy.13 = bf16[64,16,2,256]{3,2,1,0:T(2,128)(2,1)} copy(bf16[64,16,2,256]{3,2,1,0:T(2,128)(2,1)} %encoder.1) | data formatting | bytes 2097152

commit v4 on v3

--- a/solution.py
+++ b/solution.py
@@ -167,17 +167,15 @@
 
             @pl.loop(0, 18)
             def _(r):
-                for kz in range(3):
-                    mid[kz, col, r] = jnp.zeros((64, 256), BF16)
+                mid[1, col, r] = jnp.zeros((64, 256), BF16)
 
     for dy in (-1, 1):
 
         @pl.when(jnp.logical_not(has[dy]))
         def _():
             row = 0 if dy == -1 else 17
-            for kz in range(3):
-                for x in range(4):
-                    mid[kz, x, row] = jnp.zeros((64, 256), BF16)
+            for x in range(4):
+                mid[1, x, row] = jnp.zeros((64, 256), BF16)
 
     for c in range(3):
         slab[c][0] = jnp.zeros((2, CHUNKS[c][2], 128), BF16)
@@ -439,30 +437,35 @@
         mid[0, x, r] = down.astype(BF16)
         mid[2, x, r] = up.astype(BF16)
 
-    def take_sides(g):
-        for dx in (-1, 1):
-
-            @pl.when(hasx[-dx])
+    def take_sides(*groups):
+        for g in groups:
+            for dx in (-1, 1):
+
+                @pl.when(hasx[-dx])
+                def _():
+                    side_copy(dx, g).wait_recv()
+
+        for g in groups:
+            for r in range(GROUPS[g][2]):
+                spread_row(0, 1 + GROUPS[g][1] + r)
+                spread_row(3, 1 + GROUPS[g][1] + r)
+
+    def take_edges():
+        for dy in (-1, 1):
+
+            @pl.when(has[-dy])
             def _():
-                side_copy(dx, g).wait_recv()
-                for r in range(GROUPS[g][2]):
-                    spread_row(3 if dx == -1 else 0, 1 + GROUPS[g][1] + r)
-
-    def take_edges(dy):
-        row = 17 if dy == -1 else 0
-
-        @pl.when(has[-dy])
-        def _():
-            edge_copy(dy).wait_recv()
-            spread_row(1, row)
-            spread_row(2, row)
-
-        for dx in (-1, 1):
-
-            @pl.when(jnp.logical_and(has[-dy], hasx[-dx]))
-            def _():
-                corner_copy(dx, dy).wait_recv()
-                spread_row(3 if dx == -1 else 0, row)
+                edge_copy(dy).wait_recv()
+
+            for dx in (-1, 1):
+
+                @pl.when(jnp.logical_and(has[-dy], hasx[-dx]))
+                def _():
+                    corner_copy(dx, dy).wait_recv()
+
+        for x in range(4):
+            spread_row(x, 0)
+            spread_row(x, 17)
 
     def last_rows(*runs):
         res = cube_rows(mid, wb, runs, 256)
@@ -473,8 +476,7 @@
                 out[:, line, x] = res[x, r].astype(BF16)
 
     load_b.wait()
-    take_sides(0)
-    take_sides(1)
+    take_sides(0, 1)
     last_rows((7, 4))
     take_sides(2)
     last_rows((4, 3))
@@ -482,8 +484,7 @@
     last_rows((1, 3))
     take_sides(4)
     last_rows((11, 4))
-    take_edges(-1)
-    take_edges(1)
+    take_edges()
     last_rows((0, 1), (15, 1))
 
     for c in range(3):
@@ -512,10 +513,25 @@
                 corner_copy(dx, dy).wait_send()
 
 
+def hand_over(source, out, held, take, give):
+    parts = take.shape[0]
+    size = source.shape[0] // parts
+    piece = lambda ref, p: ref.at[pl.ds(p * size, size)]
+    loads = [pltpu.make_async_copy(piece(source, p), piece(held, p), take.at[p]) for p in range(parts)]
+    stores = [pltpu.make_async_copy(piece(held, p), piece(out, p), give.at[p]) for p in range(parts)]
+    for load in loads:
+        load.start()
+    for load, store in zip(loads, stores):
+        load.wait()
+        store.start()
+    for store in stores:
+        store.wait()
+
+
 def body(raw, wf, bf, ws, bs, wt, bt, wa, ba, wb, bb):
     nx, ny = lax.axis_size("gz"), lax.axis_size("xy")
     dma = pltpu.SemaphoreType.DMA
-    return pl.pallas_call(
+    out = pl.pallas_call(
         functools.partial(kernel, nx, ny),
         name="encoder",
         out_shape=jax.ShapeDtypeStruct((64, 16, 2, 256), BF16),
@@ -561,6 +577,15 @@
         wb.reshape(27 * 256, 256),
         bb.reshape(1, 256),
     )
+    return pl.pallas_call(
+        hand_over,
+        name="hand_over",
+        out_shape=jax.ShapeDtypeStruct(out.shape, BF16),
+        in_specs=[ANY],
+        out_specs=ANY,
+        scratch_shapes=[pltpu.VMEM(out.shape, BF16), dma((4,)), dma((4,))],
+        compiler_params=pltpu.CompilerParams(vmem_limit_bytes=60 << 20),
+    )(out)
 
 
 def solution(mesh):

time: 71.3 us -> 69.8 us (0.979)
  local copies, waits for them, and re-layouts: 3.13 us -> 0 us
  Pallas kernels: 68.1 us -> 69.5 us
    unnamed x1 -> x0, local copies, waits for them, and re-layouts: 3.13 us -> none
    pallas_call x0 -> x1, Pallas kernels: none -> 1.98 us  [body(): pl.pallas_call(hand_over, name='hand_over', out_shape=jax.ShapeDtypeStruc...]
where the time goes in v4:
time: 69.8 us; the launch traced here: 69.7 us
  Pallas kernels  69.5 us (100%)
    pallas_call x1, Pallas kernels, body(): pl.pallas_call(functools.partial(kernel, nx, ny), name='encoder', out_sha...  67.5 us
    pallas_call x1, Pallas kernels, body(): pl.pallas_call(hand_over, name='hand_over', out_shape=jax.ShapeDtypeStruc...  1.98 us

profile of v4, /device:TPU:16, one launch (start us, length us, event | category | flops | bytes accessed | tf_op | source)
XLA Modules:
  0.0 69.7 jit_solution(5968548245520945655)
XLA Ops:
  0.0 67.5 %encoder.1.source = bf16[64,16,2,256]{3,2,1,0:T(2,128)(2,1)} custom-call(bf16[2,128,512]{2,1,0:T(8,128)(2,1)} %raw.1, bf16[3,3,32]{2,1,0:T(4,128)(2,1)} %bitcast.16, f32[1,32]{1,0:T(1,128)} %bitcast.19, bf16[3,3,32,64]{3,2,1,0:T(8,128)(2,1)} %bitcast.15, f32[1,64]{1,0:T(1,128)} %bitcast.20, bf16[3,3,64,128]{3,2,1,0:T(8,128)(2,1)} %bitcast.14, ...), custom_call_target="tpu_custom_call" | custom-call | tf_op jit(solution)/shard_map/encoder/pallas_call | solution.py:534
  67.6 2.0 %hand_over.1 = bf16[64,16,2,256]{3,2,1,0:T(2,128)(2,1)} custom-call(bf16[64,16,2,256]{3,2,1,0:T(2,128)(2,1)} %encoder.1.source), custom_call_target="tpu_custom_call" | custom-call | tf_op jit(solution)/shard_map/hand_over/pallas_call | solution.py:580
